TPU v7x, 32 devices: a whole 2x2x4 slice. The times are simulated.
32 devices in a mesh: groups: 2 (over x), dev: 8 (over z, y), rve: 2 (over core).
Axes of the slice: x: 2, y: 2, z: 4, core: 2. Of those that a mesh axis runs over, the one named last changes fastest.
Arguments:
- phase: int32 [4, 64, 128, 128], P(('groups', 'rve'), 'dev'), parts along dimension 0, may hold values from 0 to 2
- load_case: int32 [4], P(('groups', 'rve')), parts along dimension 0, may hold values from 0 to 5
- moduli: float32 [2, 3], replicated, may hold values from 0.5 to 8
- loading_table: float32 [6, 3, 3], replicated, may hold values from -4 to 4
- w_embed: bfloat16 [1408, 768], P(('dev', 'rve')), may hold values from -0.21875 to 0.21875
- w_up: bfloat16 [3072, 1408], P(('dev', 'rve')), may hold values from -0.15625 to 0.15625
- cotangent: bfloat16 [16384, 3072], P(('groups', 'dev', 'rve')), parts along dimension 0, may hold values from -6 to 6
Outputs:
- displacement: float32 [4, 3, 64, 128, 128], P(('groups', 'rve'), None, 'dev'), parts along dimension 0
- grad_embed: float32 [2816, 768], P(('groups', 'dev', 'rve')), parts along dimension 0
- grad_up: float32 [6144, 1408], P(('groups', 'dev', 'rve')), parts along dimension 0
There are 2 independent parts, one for each index of `groups`. A program takes and returns all parts, laid end to end along the dimension named above; an argument that names none is the same for every part. Nothing has to cross between parts.
Inputs may be any that keep to these rules, and one draw needn't show every extreme that they name: `load_case`: row of loading_table for each RVE.
All inputs are finite; a program needn't handle non-finite values.
Results may differ from a plain program's by a relative error of at most 0.0069.
Values may be sent and summed in bfloat16 or wider, within the bound.
No kernel may reach another device: no remote copies, remote signals or barrier semaphores. Data moves between devices by JAX's collectives and lax.ppermute only.
A program may use at most 128 MiB of HBM per device.

v0:
```python
from functools import partial
import math

import jax
import jax.numpy as jnp
from jax import lax
from jax.experimental import pallas as pl
from jax.experimental.pallas import tpu as pltpu
from jax.sharding import PartitionSpec as P


PATCH_Y = 8
PATCH_Z = 4
SWEEPS = 4


epsilon = 1e-06
bf16 = jnp.bfloat16
f32 = jnp.float32
MIB = 1024 * 1024


def contract(left, right, left_dim, right_dim):
    return lax.dot_general(
        left, right, (((left_dim,), (right_dim,)), ((), ())), preferred_element_type=f32
    )


def exchange(value, axis, bit):
    size = lax.axis_size(axis)
    return lax.ppermute(value, axis, [(i, i ^ bit) for i in range(size)])


def shifted(plane, axis, step):
    return pltpu.roll(plane, step % plane.shape[axis], axis)


def solver_kernel(
    scalars, tables, loading, phase_ref, before_ref, after_ref, displace_ref, *rest, slab, bands, patch_y
):
    block_refs = rest[:bands]
    key, face, self_x, rdiag, force, even, odd = rest[bands:]
    halo = SWEEPS
    total = slab + 2 * halo
    phases = tables.shape[1]
    me, case = (scalars[0], scalars[2])
    first_row, grid_rows = (me * slab, slab * bands)
    ny, nz = phase_ref.shape[1:]
    iota_y = lax.broadcasted_iota(jnp.int32, (ny, nz), 0)
    iota_z = lax.broadcasted_iota(jnp.int32, (ny, nz), 1)
    pairs = [(p, q) for p in range(phases) for q in range(p, phases)]

    def blend(kind, p, q):
        here, there = (jnp.full((1, nz), tables[kind, i], f32) for i in (p, q))
        return here if p == q else 2.0 * here * there / (here + there)

    values = {(kind, p, q): blend(kind, p, q) for p, q in pairs for kind in range(2)}

    def power(labels):
        result = jnp.full(labels.shape, 1, jnp.int32)
        for p in range(1, phases):
            result = jnp.where(labels == p, 1 << p, result)
        return result

    key[pl.ds(halo, slab)] = power(phase_ref[...])
    key[pl.ds(0, halo)] = power(before_ref[...].astype(f32).astype(jnp.int32))
    key[pl.ds(halo + slab, halo)] = power(after_ref[...].astype(f32).astype(jnp.int32))

    @pl.when(first_row == 0)
    def _():
        key[halo - 1] = key[halo]

    @pl.when(first_row + slab == grid_rows)
    def _():
        key[halo + slab] = key[halo + slab - 1]

    def faces(here, there):
        code = here + there
        results = [jnp.broadcast_to(values[kind, 0, 0], code.shape) for kind in range(2)]
        for p, q in pairs[1:]:
            hit = code == ((1 << p) + (1 << q))
            for kind in range(2):
                results[kind] = jnp.where(hit, values[kind, p, q], results[kind])
        return results

    def x_faces(row, carry):
        for kind, value in enumerate(faces(key[row], key[row + 1])):
            self_x[kind, row] = value
        return carry

    lax.fori_loop(0, total - 1, x_faces, 0)

    strain = [[loading[case, c, a] for a in range(3)] for c in range(3)]

    def setup(row, carry):
        here = key[row]
        own = faces(here, here)
        above_y = jnp.where(iota_y == ny - 1, here, shifted(here, 0, -1))
        above_z = jnp.where(iota_z == nz - 1, here, shifted(here, 1, -1))
        upper_y = faces(here, above_y)
        upper_z = faces(here, above_z)
        gaps, sums = ([], [])
        for kind in range(2):
            face[kind, 0, row] = jnp.where(iota_y == ny - 1, 0.0, upper_y[kind])
            face[kind, 1, row] = jnp.where(iota_z == nz - 1, 0.0, upper_z[kind])
            lower_y = jnp.where(iota_y == 0, own[kind], shifted(upper_y[kind], 0, 1))
            lower_z = jnp.where(iota_z == 0, own[kind], shifted(upper_z[kind], 1, 1))
            upper_x, lower_x = (self_x[kind, row], self_x[kind, row - 1])
            gaps.append([upper_x - lower_x, upper_y[kind] - lower_y, upper_z[kind] - lower_z])
            sums.append([upper_x + lower_x, upper_y[kind] + lower_y, upper_z[kind] + lower_z])
        global_row = first_row + row - halo
        inside = jnp.where((global_row >= 0) & (global_row < grid_rows), 1.0, 0.0)
        for c in range(3):
            kinds = [1 if a == c else 0 for a in range(3)]
            forcing = sum(strain[c][a] * gaps[kinds[a]][a] for a in range(3))
            diagonal = sums[kinds[0]][0] + sums[kinds[1]][1] + sums[kinds[2]][2]
            inverse = inside / diagonal
            rdiag[c, row] = inverse
            force[c, row] = forcing
            even[c, row] = forcing * inverse
        return carry

    lax.fori_loop(1, total - 1, setup, 0)

    buffers = (even, odd)
    for step in range(1, SWEEPS):
        source, target = (buffers[(step - 1) % 2], buffers[step % 2])

        def sweep(row, carry, source=source, target=target, last=step == SWEEPS - 1):
            for c in range(3):
                kx, ky, kz = (1 if a == c else 0 for a in range(3))
                here = source[c, row]
                face_y = face[ky, 0, row]
                face_z = face[kz, 1, row]
                summed = (
                    force[c, row]
                    + self_x[kx, row] * source[c, row + 1]
                    + self_x[kx, row - 1] * source[c, row - 1]
                    + face_y * shifted(here, 0, -1)
                    + shifted(face_y * here, 0, 1)
                    + face_z * shifted(here, 1, -1)
                    + shifted(face_z * here, 1, 1)
                )
                value = summed * rdiag[c, row]
                target[c, row] = value
                if last:
                    displace_ref[c, row - halo] = value
            return carry

        lax.fori_loop(1 + step, total - 1 - step, sweep, 0)

    band_rows = ny // bands
    for k in range(bands):
        band = me ^ k
        at = 0
        for b in range(band_rows // patch_y):
            start = pl.multiple_of(band * band_rows + b * patch_y, patch_y)
            for c in range(3):
                for x in range(0, slab, 2):
                    pair = jnp.concatenate(
                        [displace_ref[c, x + i, pl.ds(start, patch_y), :] for i in range(2)], axis=0
                    )
                    block_refs[k][pl.ds(at, 2 * patch_y), :] = pair.astype(bf16)
                    at += 2 * patch_y


def solve(phase, before, after, scalars, tables, loading, bands):
    slab, ny, nz = phase.shape
    total = slab + 2 * SWEEPS
    rows = 3 * slab * ny // bands
    smem = pl.BlockSpec(memory_space=pltpu.SMEM)
    vmem = pl.BlockSpec(memory_space=pltpu.VMEM)
    plane = (ny, nz)
    return pl.pallas_call(
        partial(solver_kernel, slab=slab, bands=bands, patch_y=PATCH_Y),
        out_shape=[jax.ShapeDtypeStruct((3, slab) + plane, f32)]
        + [jax.ShapeDtypeStruct((rows, nz), bf16)] * bands,
        in_specs=[smem, smem, smem, vmem, vmem, vmem],
        out_specs=[vmem] * (1 + bands),
        scratch_shapes=[
            pltpu.VMEM((total,) + plane, jnp.int32),
            pltpu.VMEM((2, 2, total) + plane, f32),
            pltpu.VMEM((2, total) + plane, f32),
            pltpu.VMEM((3, total) + plane, f32),
            pltpu.VMEM((3, total) + plane, f32),
            pltpu.VMEM((3, total) + plane, f32),
            pltpu.VMEM((3, total) + plane, f32),
        ],
        compiler_params=pltpu.CompilerParams(vmem_limit_bytes=30 * MIB),
        cost_estimate=pl.CostEstimate(flops=40_000_000, bytes_accessed=4_000_000, transcendentals=0),
        name="solver",
    )(scalars, tables, loading, phase, before, after)


def feature_order(features):
    feature = jnp.arange(features, dtype=jnp.int32)
    source = (feature % PATCH_Z) * (features // PATCH_Z) + feature // PATCH_Z
    return (feature[:, None] == source[None]).astype(bf16)


def patch_kernel(scalars, *refs, slabs, bands_in):
    block_refs, (perm_ref, order_ref, out_ref, plain_ref, held) = (refs[:slabs], refs[slabs:])
    rows, lanes = block_refs[0].shape
    rows = rows // bands_in
    me = scalars[0]
    for k in range(slabs):
        held[k] = block_refs[k][...]
    group = PATCH_Z
    for g in range(slabs * bands_in // group):
        parts = []
        for j in range(group):
            b, px = divmod(group * g + j, slabs)
            parts.append(held[me ^ px, pl.ds(b * rows, rows), :])
        moved = jnp.dot(
            jnp.concatenate(parts, axis=1), perm_ref[...], preferred_element_type=f32
        ).astype(bf16)
        for z in range(group):
            out_ref[pl.ds(z * rows, rows), pl.ds(g * lanes, lanes)] = moved[:, z * lanes : (z + 1) * lanes]
    plain_ref[...] = jnp.dot(order_ref[...], out_ref[...], preferred_element_type=f32).astype(bf16)


def patchify(blocks, scalars, bands_in):
    slabs = len(blocks)
    rows, nz = blocks[0].shape
    rows = rows // bands_in
    cells = nz // PATCH_Z
    width = PATCH_Z * nz
    features = PATCH_Z * rows
    tokens = slabs * bands_in * cells
    lane = jnp.arange(width, dtype=jnp.int32)
    j, pz, z = (lane // nz, lane % nz // PATCH_Z, lane % PATCH_Z)
    perm = ((z * nz + j * cells + pz)[:, None] == lane[None]).astype(bf16)
    order = feature_order(features).T
    vmem = pl.BlockSpec(memory_space=pltpu.VMEM)
    return pl.pallas_call(
        partial(patch_kernel, slabs=slabs, bands_in=bands_in),
        out_shape=[jax.ShapeDtypeStruct((features, tokens), bf16)] * 2,
        in_specs=[pl.BlockSpec(memory_space=pltpu.SMEM)] + [vmem] * (slabs + 2),
        out_specs=[vmem] * 2,
        scratch_shapes=[pltpu.VMEM((slabs, rows * bands_in, nz), bf16)],
        compiler_params=pltpu.CompilerParams(vmem_limit_bytes=12 * MIB),
        cost_estimate=pl.CostEstimate(flops=1_000_000_000, bytes_accessed=5_000_000, transcendentals=0),
        name="patchify",
    )(scalars, *blocks, perm, order)


def turn_kernel(scalars, cot_ref, own_ref, other_ref, held):
    per, hidden = own_ref.shape[:2]
    held[...] = cot_ref[...].T
    me, core = (scalars[0], scalars[1])
    for i in range(per):
        slot = (me % per) ^ i
        start = 2 * i * hidden
        own_ref[slot] = held[pl.ds(pl.multiple_of(start + core * hidden, hidden), hidden), :]
        other_ref[slot] = held[pl.ds(pl.multiple_of(start + (1 - core) * hidden, hidden), hidden), :]


def turn(cotangent, scalars, blocks):
    tokens, hidden = cotangent.shape
    width = hidden // blocks
    per = 1
    while per * width % 128:
        per *= 2
    out = jax.ShapeDtypeStruct((blocks, width // 2, tokens), bf16)
    out_spec = pl.BlockSpec((per, width // 2, tokens), lambda i, s: ((s[0] // per) ^ i, 0, 0))
    return pl.pallas_call(
        turn_kernel,
        out_shape=[out, out],
        grid_spec=pltpu.PrefetchScalarGridSpec(
            num_scalar_prefetch=1,
            grid=(blocks // per,),
            in_specs=[pl.BlockSpec((tokens, per * width), lambda i, s: (0, i))],
            out_specs=[out_spec, out_spec],
            scratch_shapes=[pltpu.VMEM((per * width, tokens), bf16)],
        ),
        cost_estimate=pl.CostEstimate(flops=0, bytes_accessed=6_300_000, transcendentals=0),
        name="turn",
    )(scalars, cotangent)


def embed_kernel(w_ref, patch_ref, normed_ref, embed_ref, inverse_ref):
    model, tokens = embed_ref.shape
    tile = min(tokens, 256)
    for i in range(0, tokens, tile):
        cols = pl.ds(i, tile)
        value = jnp.dot(w_ref[...], patch_ref[:, cols], preferred_element_type=f32).astype(bf16)
        embed_ref[:, cols] = value
        wide = value.astype(f32)
        total = jnp.sum(wide * wide, axis=0, keepdims=True)
        inverse = lax.rsqrt(total / model + epsilon)
        inverse_ref[:, cols] = inverse
        normed_ref[:, cols] = (wide * inverse).astype(bf16)


def embed(w_all, patches):
    model, features = w_all.shape
    tokens = patches.shape[1]
    vmem = pl.BlockSpec(memory_space=pltpu.VMEM)
    return pl.pallas_call(
        embed_kernel,
        out_shape=[
            jax.ShapeDtypeStruct((model, tokens), bf16),
            jax.ShapeDtypeStruct((model, tokens), bf16),
            jax.ShapeDtypeStruct((1, tokens), f32),
        ],
        in_specs=[vmem] * 2,
        out_specs=[vmem] * 3,
        compiler_params=pltpu.CompilerParams(vmem_limit_bytes=16 * MIB),
        cost_estimate=pl.CostEstimate(
            flops=2 * model * features * tokens, bytes_accessed=6_000_000, transcendentals=0
        ),
        name="embed",
    )(w_all, patches)


def join_kernel(scalars, *refs, slots):
    mine, (theirs, order_ref, out_ref, held) = (refs[:slots], refs[slots:])
    rows = mine[0].shape[0]
    me, core = (scalars[0], scalars[1])
    for k in range(slots):
        start = (me ^ k) * (2 * rows)
        held[pl.ds(pl.multiple_of(start + core * rows, 8), rows), :] = mine[k][...].astype(f32)
        held[pl.ds(pl.multiple_of(start + (1 - core) * rows, 8), rows), :] = theirs[k].astype(f32)
    out_ref[...] = jnp.dot(held[...].astype(bf16), order_ref[...], preferred_element_type=f32).astype(bf16)


def join(mine, theirs, scalars):
    slots = len(mine)
    rows, features = mine[0].shape
    order = feature_order(features).T
    vmem = pl.BlockSpec(memory_space=pltpu.VMEM)
    return pl.pallas_call(
        partial(join_kernel, slots=slots),
        out_shape=jax.ShapeDtypeStruct((2 * slots * rows, features), bf16),
        in_specs=[pl.BlockSpec(memory_space=pltpu.SMEM)] + [vmem] * (slots + 2),
        out_specs=vmem,
        scratch_shapes=[pltpu.VMEM((2 * slots * rows, features), f32)],
        compiler_params=pltpu.CompilerParams(vmem_limit_bytes=20 * MIB),
        cost_estimate=pl.CostEstimate(flops=1_700_000_000, bytes_accessed=5_000_000, transcendentals=0),
        name="join",
    )(scalars, *mine, theirs, order)


def tail_kernel(scalars, own_ref, far_ref, embed_ref, inverse_ref, plain_ref, *rest, slots):
    mine, (theirs, total, held) = (rest[:slots], rest[slots:])
    model = own_ref.shape[0]
    rows = model // (2 * slots)
    me, core = (scalars[0], scalars[1])
    inverse = inverse_ref[...]
    summed = own_ref[...] + far_ref[...].astype(f32)
    wide = embed_ref[...].astype(f32) * inverse
    inner = jnp.sum(summed * wide, axis=0, keepdims=True) / model
    total[...] = inverse * (summed - wide * inner)
    for k in range(slots):
        start = (me ^ k) * (2 * rows)
        for part in range(2):
            source = start + (core if part == 0 else 1 - core) * rows
            held[pl.ds((part * slots + k) * rows, rows), :] = total[pl.ds(pl.multiple_of(source, 8), rows), :]
    for part in (1, 0):
        grad = contract(
            held[pl.ds(part * slots * rows, slots * rows), :].astype(bf16), plain_ref[...], 1, 1
        ).astype(bf16)
        if part:
            theirs[...] = grad
        else:
            for k in range(slots):
                mine[k][...] = grad[k * rows : (k + 1) * rows]


def tail(own_grad, far_grad, embedded, inverse, plain, scalars, slots):
    model, tokens = own_grad.shape
    features = plain.shape[0]
    rows = model // (2 * slots)
    vmem = pl.BlockSpec(memory_space=pltpu.VMEM)
    return pl.pallas_call(
        partial(tail_kernel, slots=slots),
        out_shape=[jax.ShapeDtypeStruct((rows, features), bf16)] * slots
        + [jax.ShapeDtypeStruct((slots * rows, features), bf16)],
        in_specs=[pl.BlockSpec(memory_space=pltpu.SMEM)] + [vmem] * 5,
        out_specs=[vmem] * (slots + 1),
        scratch_shapes=[pltpu.VMEM((model, tokens), f32)] * 2,
        compiler_params=pltpu.CompilerParams(vmem_limit_bytes=28 * MIB),
        cost_estimate=pl.CostEstimate(flops=1_200_000_000, bytes_accessed=9_000_000, transcendentals=0),
        name="tail",
    )(scalars, own_grad, far_grad, embedded, inverse, plain)


def gelu_slope(value):
    scale = math.sqrt(2.0 / math.pi)
    square = value * value
    bend = jnp.tanh(value * (scale + (scale * 0.044715) * square))
    return 0.5 * (1.0 + bend) + 0.5 * value * (1.0 - bend * bend) * (
        scale + (3.0 * scale * 0.044715) * square
    )


def mlp_kernel(*refs, count):
    w_refs, (normed_own, normed_far, cot_own, cot_far), outs = (
        refs[:count],
        refs[count : count + 4],
        refs[count + 4 :],
    )
    act_own, act_far, w_out = outs[:3]
    grads = outs[3:]
    hidden, model = w_refs[0].shape
    tokens = normed_own.shape[1]
    for k in range(count):
        w_out[pl.ds(k * hidden, hidden), :] = w_refs[k][...]
    tile = min(tokens, 256)
    for normed, cot, act in ((normed_own, cot_own, act_own), (normed_far, cot_far, act_far)):
        for i in range(0, tokens, tile):
            cols = pl.ds(i, tile)
            pre_act = jnp.dot(w_out[...], normed[:, cols], preferred_element_type=f32)
            cots = jnp.concatenate([cot[k, :, cols] for k in range(count)], axis=0).astype(f32)
            act[:, cols] = (cots * gelu_slope(pre_act)).astype(bf16)
    for i in range(0, model, 256):
        cols = pl.ds(i, min(256, model - i))
        value = contract(act_own[...], normed_own[cols, :], 1, 1)
        value = (value + contract(act_far[...], normed_far[cols, :], 1, 1)).astype(bf16)
        for k in range(count):
            grads[k][:, cols] = value[k * hidden : (k + 1) * hidden]


def mlp(w_slots, normed, cots, part):
    count = len(w_slots)
    hidden, model = w_slots[0].shape
    tokens = normed[0].shape[1]
    vmem = pl.BlockSpec(memory_space=pltpu.VMEM)
    cot_spec = pl.BlockSpec((count, hidden, tokens), lambda i: (part, 0, 0))
    whole = pl.BlockSpec((model, tokens), lambda i: (0, 0))
    slot = pl.BlockSpec((hidden, model), lambda i: (0, 0))
    wide = pl.BlockSpec((count * hidden, tokens), lambda i: (0, 0))
    return pl.pallas_call(
        partial(mlp_kernel, count=count),
        grid=(1,),
        out_shape=[jax.ShapeDtypeStruct((count * hidden, tokens), bf16)] * 2
        + [jax.ShapeDtypeStruct((count * hidden, model), bf16)]
        + [jax.ShapeDtypeStruct((hidden, model), bf16)] * count,
        in_specs=[slot] * count + [whole] * 2 + [cot_spec] * 2,
        out_specs=[wide] * 2 + [pl.BlockSpec((count * hidden, model), lambda i: (0, 0))] + [slot] * count,
        compiler_params=pltpu.CompilerParams(vmem_limit_bytes=30 * MIB),
        cost_estimate=pl.CostEstimate(
            flops=8 * count * hidden * model * tokens, bytes_accessed=15_000_000, transcendentals=0
        ),
    )(*w_slots, *normed, *cots)


def bits_of(size):
    return [1 << i for i in range(size.bit_length() - 1)]


def gather_slots(shard, axis, order):
    slots = {0: shard}
    for bit in order:
        for k in list(slots):
            slots[k ^ bit] = exchange(slots[k], axis, bit)
    return [slots[k] for k in range(len(slots))]


def near_slots(shard, axis):
    slots = [shard]
    for k in range(2, lax.axis_size(axis), 2):
        slots += [None, exchange(shard, axis, k)]
    pairs = [exchange(slot, axis, 1) for slot in slots[::2]]
    return [slot for both in zip(slots[::2], pairs) for slot in both]


def scatter_slots(slots, axis, order):
    live = dict(enumerate(slots))
    for bit in order:
        for k in sorted(k for k in live if k & bit):
            arrived = exchange(live.pop(k), axis, bit)
            total = live[k ^ bit].astype(f32) + arrived.astype(f32)
            live[k ^ bit] = total if bit == order[-1] else total.astype(bf16)
    return live[0]


def swap(value):
    return exchange(value, "rve", 1)


def local(phase, load_case, moduli, loading_table, w_embed, w_up, cotangent):
    phase = phase[0]
    slab, ny, _ = phase.shape
    devs = lax.axis_size("dev")
    bits = bits_of(devs)
    me = lax.axis_index("dev")
    core = lax.axis_index("rve")
    features = w_embed.shape[1]
    rows_embed = w_embed.shape[0]
    tokens = cotangent.shape[0]
    bands_in = ny // devs // PATCH_Y
    grad_scale = 1.0 / math.sqrt(tokens * devs * 2)

    small = phase.astype(bf16)
    up = [(i, i + 1) for i in range(devs - 1)]
    down = [(j, i) for i, j in up]
    before = lax.ppermute(small[slab - SWEEPS :], "dev", up)
    after = lax.ppermute(small[:SWEEPS], "dev", down)

    scalars = jnp.stack([me, core, load_case[0]]).astype(jnp.int32)
    outs = solve(phase, before, after, scalars, moduli, loading_table, devs)
    displace, blocks = (outs[0], outs[1:])

    embed_slots = near_slots(w_embed, "dev")
    w_all = join(embed_slots, swap(jnp.stack(embed_slots)), scalars)

    up_slots = gather_slots(w_up, "dev", bits[::-1])
    cot_own, cot_other = turn(cotangent, scalars, devs)
    cots = (cot_own, swap(cot_other))

    arrived = [blocks[0]] + [exchange(blocks[k], "dev", k) for k in range(1, devs)]
    patches, plain = patchify(arrived, scalars, bands_in)
    far_patches = swap(patches)
    normed_own, embedded, inverse_rms = embed(w_all, patches)
    normed_far, _, _ = embed(w_all, far_patches)

    half = devs // 2
    grads = [None] * devs
    own_parts, far_parts, w_parts = ([], [], [])
    for part in (1, 0):
        act_own, act_far, w_part, *grads[part * half : (part + 1) * half] = mlp(
            up_slots[part * half : (part + 1) * half], (normed_own, normed_far), cots, part
        )
        own_parts.append(act_own)
        far_parts.append(act_far)
        w_parts.append(w_part)
    grad_up = scatter_slots(grads, "dev", bits) * grad_scale

    far_grad = sum(contract(w, act, 0, 0) for w, act in zip(w_parts, far_parts)).astype(bf16)
    partner = swap(far_grad)
    own_grad = sum(contract(w, act, 0, 0) for w, act in zip(w_parts, own_parts))
    *mine, yours = tail(own_grad, partner, embedded, inverse_rms, plain, scalars, devs)
    arrived = swap(yours).reshape(devs, rows_embed, features)
    mine = [(m.astype(f32) + arrived[k].astype(f32)).astype(bf16) for k, m in enumerate(mine)]
    grad_embed = scatter_slots(mine, "dev", bits[1::-1] + bits[2:]) * grad_scale
    return (displace[None], grad_embed, grad_up)


def solution(mesh):
    return jax.shard_map(
        local,
        mesh=mesh,
        in_specs=(
            P(("groups", "rve"), "dev", None, None),
            P(("groups", "rve")),
            P(),
            P(),
            P(("dev", "rve"), None),
            P(("dev", "rve"), None),
            P(("groups", "dev", "rve"), None),
        ),
        out_specs=(
            P(("groups", "rve"), None, "dev", None, None),
            P(("groups", "dev", "rve"), None),
            P(("groups", "dev", "rve"), None),
        ),
        check_vma=False,
    )
```

profile of v0, /device:TPU:0, one launch (start us, length us, event | category | flops | bytes accessed | tf_op | source)
XLA Modules:
  0.0 255.1 jit_solution(10256765311962594245)
XLA Ops:
  0.6 5.1 %collective-permute-start.11 = (bf16[88,768]{1,0:T(8,128)(2,1)}, bf16[88,768]{1,0:T(8,128)(2,1)S(1)}, u32[]{:S(2)}, u32[]{:S(2)}) collective-permute-start(bf16[88,768]{1,0:T(8,128)(2,1)} %refs_0_.2), channel_id=1, source_target_pairs={{0,12},{2,14},{4,8},{6,10},{8,4},{10,6},{12,0},{14,2},{1,13},{3,15... | collective-permute-start | bytes 405512 | tf_op jit(solution)/shard_map/ppermute | solution.py:31
  12.5 7.5 %turn.1 = (bf16[8,192,512]{2,1,0:T(8,128)(2,1)}, bf16[8,192,512]{2,1,0:T(8,128)(2,1)}) custom-call(s32[3]{0:T(128)} %pad_add_fusion.scalars, bf16[512,3072]{1,0:T(8,128)(2,1)} %cot_ref.1), custom_call_target="tpu_custom_call" | custom-call | bytes 6300000 | tf_op jit(solution)/shard_map/turn/pallas_call | solution.py:266
  20.7 4.5 %collective-permute-start = (bf16[4,128,128]{2,1,0:T(8,128)(2,1)}, bf16[4,128,128]{2,1,0:T(8,128)(2,1)S(1)}, u32[]{:S(2)}, u32[]{:S(2)}) collective-permute-start(bf16[4,128,128]{2,1,0:T(8,128)(2,1)} %get-tuple-element.90), channel_id=1, source_target_pairs={{0,2},{2,4},{4,6},{6,8},{8,10},{10,12},{12,14},{1,3},{3,5},{5,7},{... | collective-permute-start | bytes 393224 | tf_op jit(solution)/shard_map/ppermute | solution.py:498
  34.1 2.7 %collective-permute-done.10.refs_5_ = bf16[88,768]{1,0:T(8,128)(2,1)S(1)} collective-permute-done((bf16[88,768]{1,0:T(8,128)(2,1)S(1)}, bf16[88,768]{1,0:T(8,128)(2,1)S(1)}, u32[]{:S(2)}, u32[]{:S(2)}) %collective-permute-start.10) | collective-permute-done | bytes 135200 | tf_op jit(solution)/shard_map/ppermute | solution.py:31
  38.9 13.3 %solver.1 = (f32[3,8,128,128]{3,2,1,0:T(8,128)}, bf16[384,128]{1,0:T(8,128)(2,1)S(1)}, bf16[384,128]{1,0:T(8,128)(2,1)S(1)}, bf16[384,128]{1,0:T(8,128)(2,1)S(1)...) custom-call(s32[3]{0:T(128)S(1)} %copy-done.2, ...), custom_call_target="tpu_custom_call" | custom-call | flops 40000000 | bytes 4000000 | tf_op jit(solution)/shard_map/solver/pallas_call | solution.py:174
  57.4 2.9 %collective-permute-start.17 = (bf16[384,128]{1,0:T(8,128)(2,1)S(1)}, bf16[384,128]{1,0:T(8,128)(2,1)S(1)}, u32[]{:S(2)}, u32[]{:S(2)}) collective-permute-start(bf16[384,128]{1,0:T(8,128)(2,1)S(1)} %get-tuple-element.48), channel_id=1, source_target_pairs={{0,8},{2,10},{4,12},{6,14},{8,0},{10,2},{12,4},{14,6},{1,9},{3,11}... | collective-permute-start | bytes 294920 | tf_op jit(solution)/shard_map/ppermute | solution.py:31
  64.9 4.9 %collective-permute-done.17.refs_4_ = bf16[384,128]{1,0:T(8,128)(2,1)S(1)} collective-permute-done((bf16[384,128]{1,0:T(8,128)(2,1)S(1)}, bf16[384,128]{1,0:T(8,128)(2,1)S(1)}, u32[]{:S(2)}, u32[]{:S(2)}) %collective-permute-start.17) | collective-permute-done | bytes 98336 | tf_op jit(solution)/shard_map/ppermute | solution.py:31
  72.4 12.7 %collective-permute-start.24 = (bf16[192,1408]{1,0:T(8,128)(2,1)S(1)}, bf16[192,1408]{1,0:T(8,128)(2,1)S(1)}, u32[]{:S(2)}, u32[]{:S(2)}) collective-permute-start(bf16[192,1408]{1,0:T(8,128)(2,1)S(1)} %copy-done.5), channel_id=1, source_target_pairs={{0,4},{2,6},{4,0},{6,2},{8,12},{10,14},{12,8},{14,10},{1,5},{3,7},... | collective-permute-start | bytes 1622024 | tf_op jit(solution)/shard_map/ppermute | solution.py:31
  87.7 23.1 %collective-permute-done.20.refs_7_ = bf16[384,128]{1,0:T(8,128)(2,1)S(1)} collective-permute-done((bf16[384,128]{1,0:T(8,128)(2,1)S(1)}, bf16[384,128]{1,0:T(8,128)(2,1)S(1)}, u32[]{:S(2)}, u32[]{:S(2)}) %collective-permute-start.20) | collective-permute-done | bytes 98336 | tf_op jit(solution)/shard_map/ppermute | solution.py:31
  115.1 3.4 %join.1.w_ref = bf16[1408,768]{1,0:T(8,128)(2,1)S(1)} custom-call(s32[3]{0:T(128)S(1)} %copy-done.2, bf16[88,768]{1,0:T(8,128)(2,1)S(1)} %copy-done.1, bf16[88,768]{1,0:T(8,128)(2,1)S(1)} %collective-permute-done.6.refs_1_, bf16[88,768]{1,0:T(8,128)(2,1)S(1)} %collective-permute-done.7.refs_2_, bf16[88,768]{1,0:T(8,128)(2,1)S(1)} %collective-permute-done.8.refs_3_, ...), custom_call_target="tpu_custom_call" | custom-call | flops 1700000000 | bytes 5000000 | tf_op jit(solution)/shard_map/join/pallas_call | solution.py:332
  121.5 6.0 %collective-permute-done.4.refs_2_ = bf16[192,1408]{1,0:T(8,128)(2,1)S(1)} collective-permute-done((bf16[192,1408]{1,0:T(8,128)(2,1)S(1)}, bf16[192,1408]{1,0:T(8,128)(2,1)S(1)}, u32[]{:S(2)}, u32[]{:S(2)}) %collective-permute-start.4) | collective-permute-done | bytes 540704 | tf_op jit(solution)/shard_map/ppermute | solution.py:31
  128.8 2.7 %embed.3 = (bf16[1408,512]{1,0:T(8,128)(2,1)S(1)}, bf16[1408,512]{1,0:T(8,128)(2,1)}, f32[1,512]{1,0:T(1,128)}) custom-call(bf16[1408,768]{1,0:T(8,128)(2,1)S(1)} %join.1.w_ref, bf16[768,512]{1,0:T(8,128)(2,1)S(1)} %collective-permute-done.21.patch_ref), custom_call_target="tpu_custom_call" | custom-call | flops 1107296256 | bytes 6000000 | tf_op jit(solution)/shard_map/embed/pallas_call | solution.py:299
  131.5 8.3 %collective-permute-done.25.refs_3_ = bf16[192,1408]{1,0:T(8,128)(2,1)S(1)} collective-permute-done((bf16[192,1408]{1,0:T(8,128)(2,1)S(1)}, bf16[192,1408]{1,0:T(8,128)(2,1)S(1)}, u32[]{:S(2)}, u32[]{:S(2)}) %collective-permute-start.25) | collective-permute-done | bytes 540704 | tf_op jit(solution)/shard_map/ppermute | solution.py:31
  139.8 6.1 %shard_map.95 = (bf16[768,512]{1,0:T(8,128)(2,1)S(1)}, bf16[768,512]{1,0:T(8,128)(2,1)S(1)}, bf16[768,1408]{1,0:T(8,128)(2,1)S(1)}, bf16[192,1408]{1,0:T(8,128)(...) custom-call(bf16[192,1408]{1,0:T(8,128)(2,1)S(1)} %copy-done.5, ...), custom_call_target="tpu_custom_call" | custom-call | flops 4429185024 | bytes 15000000 | tf_op jit(solution)/shard_map/pallas_call | solution.py:433
  147.4 4.0 %collective-permute-done.3.refs_1_ = bf16[192,1408]{1,0:T(8,128)(2,1)S(1)} collective-permute-done((bf16[192,1408]{1,0:T(8,128)(2,1)S(1)}, bf16[192,1408]{1,0:T(8,128)(2,1)S(1)}, u32[]{:S(2)}, u32[]{:S(2)}) %collective-permute-start.3) | collective-permute-done | bytes 540704 | tf_op jit(solution)/shard_map/ppermute | solution.py:31
  151.3 11.0 %collective-permute-done.5.refs_3_ = bf16[192,1408]{1,0:T(8,128)(2,1)S(1)} collective-permute-done((bf16[192,1408]{1,0:T(8,128)(2,1)S(1)}, bf16[192,1408]{1,0:T(8,128)(2,1)S(1)}, u32[]{:S(2)}, u32[]{:S(2)}) %collective-permute-start.5) | collective-permute-done | bytes 540704 | tf_op jit(solution)/shard_map/ppermute | solution.py:31
  162.4 6.1 %shard_map.94 = (bf16[768,512]{1,0:T(8,128)(2,1)S(1)}, bf16[768,512]{1,0:T(8,128)(2,1)S(1)}, bf16[768,1408]{1,0:T(8,128)(2,1)S(1)}, bf16[192,1408]{1,0:T(8,128)(...) custom-call(bf16[192,1408]{1,0:T(8,128)(2,1)S(1)} %collective-permute-done.2.r, ...), custom_call_target="tpu_custom_call" | custom-call | flops 4429185024 | bytes 15000000 | tf_op jit(solution)/shard_map/pallas_call | solution.py:433
  173.9 3.4 %tail.1 = (bf16[88,768]{1,0:T(8,128)(2,1)S(1)}, bf16[88,768]{1,0:T(8,128)(2,1)S(1)}, bf16[88,768]{1,0:T(8,128)(2,1)S(1)}, bf16[88,768]{1,0:T(8,128)(2,1)S(1)}, b...) custom-call(s32[3]{0:T(128)S(1)} %copy-done.2, ...), custom_call_target="tpu_custom_call" | custom-call | flops 1200000000 | bytes 9000000 | tf_op jit(solution)/shard_map/tail/pallas_call | solution.py:375
  180.4 6.1 %collective-permute-done.39 = bf16[192,1408]{1,0:T(8,128)(2,1)S(1)} collective-permute-done((bf16[192,1408]{1,0:T(8,128)(2,1)S(1)}, bf16[192,1408]{1,0:T(8,128)(2,1)S(1)}, u32[]{:S(2)}, u32[]{:S(2)}) %collective-permute-start.39) | collective-permute-done | bytes 540704 | tf_op jit(solution)/shard_map/ppermute | solution.py:31
  188.3 9.7 %collective-permute-done.36 = bf16[192,1408]{1,0:T(8,128)(2,1)S(1)} collective-permute-done((bf16[192,1408]{1,0:T(8,128)(2,1)S(1)}, bf16[192,1408]{1,0:T(8,128)(2,1)S(1)}, u32[]{:S(2)}, u32[]{:S(2)}) %collective-permute-start.36) | collective-permute-done | bytes 540704 | tf_op jit(solution)/shard_map/ppermute | solution.py:31
  200.5 20.3 %collective-permute-done.38 = bf16[192,1408]{1,0:T(8,128)(2,1)S(1)} collective-permute-done((bf16[192,1408]{1,0:T(8,128)(2,1)S(1)}, bf16[192,1408]{1,0:T(8,128)(2,1)S(1)}, u32[]{:S(2)}, u32[]{:S(2)}) %collective-permute-start.38) | collective-permute-done | bytes 540704 | tf_op jit(solution)/shard_map/ppermute | solution.py:31
  223.1 4.0 %collective-permute-done.29 = bf16[88,768]{1,0:T(8,128)(2,1)S(1)} collective-permute-done((bf16[88,768]{1,0:T(8,128)(2,1)S(1)}, bf16[88,768]{1,0:T(8,128)(2,1)S(1)}, u32[]{:S(2)}, u32[]{:S(2)}) %collective-permute-start.29) | collective-permute-done | bytes 135200 | tf_op jit(solution)/shard_map/ppermute | solution.py:31
  228.5 11.0 %collective-permute-done.31 = bf16[88,768]{1,0:T(8,128)(2,1)S(1)} collective-permute-done((bf16[88,768]{1,0:T(8,128)(2,1)S(1)}, bf16[88,768]{1,0:T(8,128)(2,1)S(1)}, u32[]{:S(2)}, u32[]{:S(2)}) %collective-permute-start.31) | collective-permute-done | bytes 135200 | tf_op jit(solution)/shard_map/ppermute | solution.py:31
  243.5 8.1 %collective-permute-done.41 = bf16[192,1408]{1,0:T(8,128)(2,1)S(1)} collective-permute-done((bf16[192,1408]{1,0:T(8,128)(2,1)S(1)}, bf16[192,1408]{1,0:T(8,128)(2,1)S(1)}, u32[]{:S(2)}, u32[]{:S(2)}) %collective-permute-start.41) | collective-permute-done | bytes 540704 | tf_op jit(solution)/shard_map/ppermute | solution.py:31
  (111 shorter events, 66.8 us)
Async XLA Ops:
  0.6 27.2 %collective-permute-start.11 = (bf16[88,768]{1,0:T(8,128)(2,1)}, bf16[88,768]{1,0:T(8,128)(2,1)S(1)}, u32[]{:S(2)}, u32[]{:S(2)}) collective-permute-start(bf16[88,768]{1,0:T(8,128)(2,1)} %refs_0_.2), channel_id=1, source_target_pairs={{0,12},{2,14},{4,8},{6,10},{8,4},{10,6},{12,0},{14,2},{1,13},{3,15... | collective-permute-start | bytes 405512 | tf_op jit(solution)/shard_map/ppermute | solution.py:31
  5.8 22.1 %collective-permute-start.9 = (bf16[88,768]{1,0:T(8,128)(2,1)}, bf16[88,768]{1,0:T(8,128)(2,1)S(1)}, u32[]{:S(2)}, u32[]{:S(2)}) collective-permute-start(bf16[88,768]{1,0:T(8,128)(2,1)} %refs_0_.2), channel_id=1, source_target_pairs={{0,8},{2,10},{4,12},{6,14},{8,0},{10,2},{12,4},{14,6},{1,9},{3,11}... | collective-permute-start | bytes 405512 | tf_op jit(solution)/shard_map/ppermute | solution.py:31
  6.4 18.8 %collective-permute-start.6 = (bf16[88,768]{1,0:T(8,128)(2,1)}, bf16[88,768]{1,0:T(8,128)(2,1)S(1)}, u32[]{:S(2)}, u32[]{:S(2)}) collective-permute-start(bf16[88,768]{1,0:T(8,128)(2,1)} %refs_0_.2), channel_id=1, source_target_pairs={{0,2},{2,0},{4,6},{6,4},{8,10},{10,8},{12,14},{14,12},{1,3},{3,1},... | collective-permute-start | bytes 405512 | tf_op jit(solution)/shard_map/ppermute | solution.py:31
  9.9 29.0 %collective-permute-start.1 = (bf16[4,128,128]{2,1,0:T(8,128)(2,1)}, bf16[4,128,128]{2,1,0:T(8,128)(2,1)S(1)}, u32[]{:S(2)}, u32[]{:S(2)}) collective-permute-start(bf16[4,128,128]{2,1,0:T(8,128)(2,1)} %get-tuple-element.89), channel_id=1, source_target_pairs={{2,0},{4,2},{6,4},{8,6},{10,8},{12,10},{14,12},{3,1},{5,3},{7,5},{... | collective-permute-start | bytes 393224 | tf_op jit(solution)/shard_map/ppermute | solution.py:499
  20.7 18.2 %collective-permute-start = (bf16[4,128,128]{2,1,0:T(8,128)(2,1)}, bf16[4,128,128]{2,1,0:T(8,128)(2,1)S(1)}, u32[]{:S(2)}, u32[]{:S(2)}) collective-permute-start(bf16[4,128,128]{2,1,0:T(8,128)(2,1)} %get-tuple-element.90), channel_id=1, source_target_pairs={{0,2},{2,4},{4,6},{6,8},{8,10},{10,12},{12,14},{1,3},{3,5},{5,7},{... | collective-permute-start | bytes 393224 | tf_op jit(solution)/shard_map/ppermute | solution.py:498
  27.9 111.9 %collective-permute-start.22 = (bf16[8,192,512]{2,1,0:T(8,128)(2,1)}, bf16[8,192,512]{2,1,0:T(8,128)(2,1)S(1)}, u32[]{:S(2)}, u32[]{:S(2)}) collective-permute-start(bf16[8,192,512]{2,1,0:T(8,128)(2,1)} %get-tuple-element.56), channel_id=1, source_target_pairs={{0,1},{1,0},{2,3},{3,2},{4,5},{5,4},{6,7},{7,6},{8,9},{9,8},{10,11... | collective-permute-start | bytes 4718600 | tf_op jit(solution)/shard_map/ppermute | solution.py:31
  38.8 75.5 %collective-permute-start.13 = (bf16[8,88,768]{2,1,0:T(8,128)(2,1)}, bf16[8,88,768]{2,1,0:T(8,128)(2,1)}, u32[]{:S(2)}, u32[]{:S(2)}) collective-permute-start(bf16[8,88,768]{2,1,0:T(8,128)(2,1)} %bitcast_dynamic-update-slice_fusion), channel_id=1, source_target_pairs={{0,1},{1,0},{2,3},{3,2},{4,5},{5,4},{6,7},{7,6},{8,9},{9,8},{10,11... | collective-permute-start | bytes 3244040 | tf_op jit(solution)/shard_map/ppermute | solution.py:31
  62.1 23.0 %collective-permute-start.19 = (bf16[384,128]{1,0:T(8,128)(2,1)S(1)}, bf16[384,128]{1,0:T(8,128)(2,1)S(1)}, u32[]{:S(2)}, u32[]{:S(2)}) collective-permute-start(bf16[384,128]{1,0:T(8,128)(2,1)S(1)} %get-tuple-element.50), channel_id=1, source_target_pairs={{0,12},{2,14},{4,8},{6,10},{8,4},{10,6},{12,0},{14,2},{1,13},{3,15... | collective-permute-start | bytes 294920 | tf_op jit(solution)/shard_map/ppermute | solution.py:31
  69.7 43.1 %collective-permute-start.2 = (bf16[192,1408]{1,0:T(8,128)(2,1)S(1)}, bf16[192,1408]{1,0:T(8,128)(2,1)S(1)}, u32[]{:S(2)}, u32[]{:S(2)}) collective-permute-start(bf16[192,1408]{1,0:T(8,128)(2,1)S(1)} %copy-done.5), channel_id=1, source_target_pairs={{0,8},{2,10},{4,12},{6,14},{8,0},{10,2},{12,4},{14,6},{1,9},{3,11}... | collective-permute-start | bytes 1622024 | tf_op jit(solution)/shard_map/ppermute | solution.py:31
  72.4 40.5 %collective-permute-start.24 = (bf16[192,1408]{1,0:T(8,128)(2,1)S(1)}, bf16[192,1408]{1,0:T(8,128)(2,1)S(1)}, u32[]{:S(2)}, u32[]{:S(2)}) collective-permute-start(bf16[192,1408]{1,0:T(8,128)(2,1)S(1)} %copy-done.5), channel_id=1, source_target_pairs={{0,4},{2,6},{4,0},{6,2},{8,12},{10,14},{12,8},{14,10},{1,5},{3,7},... | collective-permute-start | bytes 1622024 | tf_op jit(solution)/shard_map/ppermute | solution.py:31
  85.1 25.7 %collective-permute-start.20 = (bf16[384,128]{1,0:T(8,128)(2,1)S(1)}, bf16[384,128]{1,0:T(8,128)(2,1)S(1)}, u32[]{:S(2)}, u32[]{:S(2)}) collective-permute-start(bf16[384,128]{1,0:T(8,128)(2,1)S(1)} %get-tuple-element.51), channel_id=1, source_target_pairs={{0,14},{2,12},{4,10},{6,8},{8,6},{10,4},{12,2},{14,0},{1,15},{3,13... | collective-permute-start | bytes 294920 | tf_op jit(solution)/shard_map/ppermute | solution.py:31
  113.0 18.5 %collective-permute-start.23 = (bf16[192,1408]{1,0:T(8,128)(2,1)S(1)}, bf16[192,1408]{1,0:T(8,128)(2,1)S(1)}, u32[]{:S(2)}, u32[]{:S(2)}) collective-permute-start(bf16[192,1408]{1,0:T(8,128)(2,1)S(1)} %copy-done.5), channel_id=1, source_target_pairs={{0,2},{2,0},{4,6},{6,4},{8,10},{10,8},{12,14},{14,12},{1,3},{3,1},... | collective-permute-start | bytes 1622024 | tf_op jit(solution)/shard_map/ppermute | solution.py:31
  114.3 25.5 %collective-permute-start.25 = (bf16[192,1408]{1,0:T(8,128)(2,1)S(1)}, bf16[192,1408]{1,0:T(8,128)(2,1)S(1)}, u32[]{:S(2)}, u32[]{:S(2)}) collective-permute-start(bf16[192,1408]{1,0:T(8,128)(2,1)S(1)} %collective-permute-done.24.refs_2_), channel_id=1, source_target_pairs={{0,2},{2,0},{4,6},{6,4},{8,10},{10,8},{12,14},{14,12},{1,3},{3,1},... | collective-permute-start | bytes 1622024 | tf_op jit(solution)/shard_map/ppermute | solution.py:31
  120.2 31.1 %collective-permute-start.3 = (bf16[192,1408]{1,0:T(8,128)(2,1)S(1)}, bf16[192,1408]{1,0:T(8,128)(2,1)S(1)}, u32[]{:S(2)}, u32[]{:S(2)}) collective-permute-start(bf16[192,1408]{1,0:T(8,128)(2,1)S(1)} %collective-permute-done.2.refs_0_), channel_id=1, source_target_pairs={{0,2},{2,0},{4,6},{6,4},{8,10},{10,8},{12,14},{14,12},{1,3},{3,1},... | collective-permute-start | bytes 1622024 | tf_op jit(solution)/shard_map/ppermute | solution.py:31
  127.5 34.8 %collective-permute-start.5 = (bf16[192,1408]{1,0:T(8,128)(2,1)S(1)}, bf16[192,1408]{1,0:T(8,128)(2,1)S(1)}, u32[]{:S(2)}, u32[]{:S(2)}) collective-permute-start(bf16[192,1408]{1,0:T(8,128)(2,1)S(1)} %collective-permute-done.4.refs_2_), channel_id=1, source_target_pairs={{0,2},{2,0},{4,6},{6,4},{8,10},{10,8},{12,14},{14,12},{1,3},{3,1},... | collective-permute-start | bytes 1622024 | tf_op jit(solution)/shard_map/ppermute | solution.py:31
  177.3 22.6 %collective-permute-start.27 = (bf16[704,768]{1,0:T(8,128)(2,1)S(1)}, bf16[704,768]{1,0:T(8,128)(2,1)S(1)}, u32[]{:S(2)}, u32[]{:S(2)}) collective-permute-start(bf16[704,768]{1,0:T(8,128)(2,1)S(1)} %get-tuple-element.67), channel_id=1, source_target_pairs={{0,1},{1,0},{2,3},{3,2},{4,5},{5,4},{6,7},{7,6},{8,9},{9,8},{10,11... | collective-permute-start | bytes 3244040 | tf_op jit(solution)/shard_map/ppermute | solution.py:31
  177.6 20.4 %collective-permute-start.36 = (bf16[192,1408]{1,0:T(8,128)(2,1)S(1)}, bf16[192,1408]{1,0:T(8,128)(2,1)S(1)}, u32[]{:S(2)}, u32[]{:S(2)}) collective-permute-start(bf16[192,1408]{1,0:T(8,128)(2,1)S(1)} %get-tuple-element.78), channel_id=1, source_target_pairs={{0,2},{2,0},{4,6},{6,4},{8,10},{10,8},{12,14},{14,12},{1,3},{3,1},... | collective-permute-start | bytes 1622024 | tf_op jit(solution)/shard_map/ppermute | solution.py:31
  178.3 65.0 %collective-permute-start.35 = (bf16[192,1408]{1,0:T(8,128)(2,1)S(1)}, bf16[192,1408]{1,0:T(8,128)(2,1)S(1)}, u32[]{:S(2)}, u32[]{:S(2)}) collective-permute-start(bf16[192,1408]{1,0:T(8,128)(2,1)S(1)} %get-tuple-element.76), channel_id=1, source_target_pairs={{0,2},{2,0},{4,6},{6,4},{8,10},{10,8},{12,14},{14,12},{1,3},{3,1},... | collective-permute-start | bytes 1622024 | tf_op jit(solution)/shard_map/ppermute | solution.py:31
  179.6 41.1 %collective-permute-start.38 = (bf16[192,1408]{1,0:T(8,128)(2,1)S(1)}, bf16[192,1408]{1,0:T(8,128)(2,1)S(1)}, u32[]{:S(2)}, u32[]{:S(2)}) collective-permute-start(bf16[192,1408]{1,0:T(8,128)(2,1)S(1)} %get-tuple-element.80), channel_id=1, source_target_pairs={{0,2},{2,0},{4,6},{6,4},{8,10},{10,8},{12,14},{14,12},{1,3},{3,1},... | collective-permute-start | bytes 1622024 | tf_op jit(solution)/shard_map/ppermute | solution.py:31
  186.6 35.8 %collective-permute-start.40 = (bf16[192,1408]{1,0:T(8,128)(2,1)S(1)}, bf16[192,1408]{1,0:T(8,128)(2,1)S(1)}, u32[]{:S(2)}, u32[]{:S(2)}) collective-permute-start(bf16[192,1408]{1,0:T(8,128)(2,1)S(1)} %add_convert_fusion.1), channel_id=1, source_target_pairs={{0,4},{2,6},{4,0},{6,2},{8,12},{10,14},{12,8},{14,10},{1,5},{3,7},... | collective-permute-start | bytes 1622024 | tf_op jit(solution)/shard_map/ppermute | solution.py:31
  198.1 45.3 %collective-permute-start.37 = (bf16[192,1408]{1,0:T(8,128)(2,1)S(1)}, bf16[192,1408]{1,0:T(8,128)(2,1)S(1)}, u32[]{:S(2)}, u32[]{:S(2)}) collective-permute-start(bf16[192,1408]{1,0:T(8,128)(2,1)S(1)} %add_convert_fusion.4), channel_id=1, source_target_pairs={{0,4},{2,6},{4,0},{6,2},{8,12},{10,14},{12,8},{14,10},{1,5},{3,7},... | collective-permute-start | bytes 1622024 | tf_op jit(solution)/shard_map/ppermute | solution.py:31
  200.0 22.7 %collective-permute-start.32 = (bf16[88,768]{1,0:T(8,128)(2,1)S(1)}, bf16[88,768]{1,0:T(8,128)(2,1)S(1)}, u32[]{:S(2)}, u32[]{:S(2)}) collective-permute-start(bf16[88,768]{1,0:T(8,128)(2,1)S(1)} %get-tuple-element.84), channel_id=1, source_target_pairs={{0,4},{2,6},{4,0},{6,2},{8,12},{10,14},{12,8},{14,10},{1,5},{3,7},... | collective-permute-start | bytes 405512 | tf_op jit(solution)/shard_map/ppermute | solution.py:31
  222.6 28.9 %collective-permute-start.41 = (bf16[192,1408]{1,0:T(8,128)(2,1)S(1)}, bf16[192,1408]{1,0:T(8,128)(2,1)S(1)}, u32[]{:S(2)}, u32[]{:S(2)}) collective-permute-start(bf16[192,1408]{1,0:T(8,128)(2,1)S(1)} %add_convert_fusion), channel_id=1, source_target_pairs={{0,8},{2,10},{4,12},{6,14},{8,0},{10,2},{12,4},{14,6},{1,9},{3,11}... | collective-permute-start | bytes 1622024 | tf_op jit(solution)/shard_map/ppermute | solution.py:31
  222.7 16.9 %collective-permute-start.31 = (bf16[88,768]{1,0:T(8,128)(2,1)S(1)}, bf16[88,768]{1,0:T(8,128)(2,1)S(1)}, u32[]{:S(2)}, u32[]{:S(2)}) collective-permute-start(bf16[88,768]{1,0:T(8,128)(2,1)S(1)} %get-tuple-element.85), channel_id=1, source_target_pairs={{0,4},{2,6},{4,0},{6,2},{8,12},{10,14},{12,8},{14,10},{1,5},{3,7},... | collective-permute-start | bytes 405512 | tf_op jit(solution)/shard_map/ppermute | solution.py:31
  (25 other events, 311.5 us)
where the time goes:
time: 256 us; the launch traced here: 255 us
  waiting for transfers between devices  126 us (49%)
  starting transfers between devices  64.4 us (25%)
  Pallas kernels  46 us (18%)
  local copies, waits for them, and re-layouts  6.19 us (2%)
  matrix products  5.61 us (2%)
  other arithmetic  5.04 us (2%)
    ppermute x40, waiting for transfers between devices, exchange(): return lax.ppermute(value, axis, [(i, i ^ bit) for i in range(size)])  126 us
    ppermute x40, starting transfers between devices, exchange(): return lax.ppermute(value, axis, [(i, i ^ bit) for i in range(size)])  58.6 us
    pallas_call x1, Pallas kernels, solve(): pl.pallas_call(partial(solver_kernel, slab=slab, bands=bands, patch_y=PAT...  13.3 us
    pallas_call x2, Pallas kernels, mlp(): pl.pallas_call(partial(mlp_kernel, count=count), grid=(1,), out_shape=[ja...  12.1 us
    pallas_call x1, Pallas kernels, turn(): pl.pallas_call(turn_kernel, out_shape=[out, out], grid_spec=pltpu.Prefetc...  7.49 us
    dot_general x4, matrix products, contract(): lax.dot_general(left, right, (((left_dim,), (right_dim,)), ((), ())), pre...  5.61 us
  transfers between devices with their start and end apart: 42, of which 17 were waited for; matrix products, arithmetic and copies ran while one was open for 6% of the time, Pallas kernels for 16%

commit v1 on v0

--- a/solution.py
+++ b/solution.py
@@ -255,26 +255,29 @@
         other_ref[slot] = held[pl.ds(pl.multiple_of(start + (1 - core) * hidden, hidden), hidden), :]
 
 
-def turn(cotangent, scalars, blocks):
+def turn(cotangent, scalars, blocks, part):
     tokens, hidden = cotangent.shape
     width = hidden // blocks
     per = 1
     while per * width % 128:
         per *= 2
-    out = jax.ShapeDtypeStruct((blocks, width // 2, tokens), bf16)
-    out_spec = pl.BlockSpec((per, width // 2, tokens), lambda i, s: ((s[0] // per) ^ i, 0, 0))
+    steps = blocks // 2 // per
+    out = jax.ShapeDtypeStruct((blocks // 2, width // 2, tokens), bf16)
+    out_spec = pl.BlockSpec((per, width // 2, tokens), lambda i, s: (i, 0, 0))
     return pl.pallas_call(
         turn_kernel,
         out_shape=[out, out],
         grid_spec=pltpu.PrefetchScalarGridSpec(
             num_scalar_prefetch=1,
-            grid=(blocks // per,),
-            in_specs=[pl.BlockSpec((tokens, per * width), lambda i, s: (0, i))],
+            grid=(steps,),
+            in_specs=[
+                pl.BlockSpec((tokens, per * width), lambda i, s: (0, (s[0] // per) ^ (part * steps + i)))
+            ],
             out_specs=[out_spec, out_spec],
             scratch_shapes=[pltpu.VMEM((per * width, tokens), bf16)],
         ),
-        cost_estimate=pl.CostEstimate(flops=0, bytes_accessed=6_300_000, transcendentals=0),
-        name="turn",
+        compiler_params=pltpu.CompilerParams(vmem_limit_bytes=16 * MIB),
+        cost_estimate=pl.CostEstimate(flops=0, bytes_accessed=3_200_000, transcendentals=0),
     )(scalars, cotangent)
 
 
@@ -313,32 +316,31 @@
     )(w_all, patches)
 
 
-def join_kernel(scalars, *refs, slots):
-    mine, (theirs, order_ref, out_ref, held) = (refs[:slots], refs[slots:])
-    rows = mine[0].shape[0]
+def join_kernel(scalars, even, odd, even_far, odd_far, order_ref, out_ref, held):
+    half, rows = even.shape[:2]
     me, core = (scalars[0], scalars[1])
-    for k in range(slots):
+    for k in range(2 * half):
         start = (me ^ k) * (2 * rows)
-        held[pl.ds(pl.multiple_of(start + core * rows, 8), rows), :] = mine[k][...].astype(f32)
-        held[pl.ds(pl.multiple_of(start + (1 - core) * rows, 8), rows), :] = theirs[k].astype(f32)
+        for part, source in ((core, (even, odd)), (1 - core, (even_far, odd_far))):
+            at = pl.multiple_of(start + part * rows, 8)
+            held[pl.ds(at, rows), :] = source[k & 1][k // 2].astype(f32)
     out_ref[...] = jnp.dot(held[...].astype(bf16), order_ref[...], preferred_element_type=f32).astype(bf16)
 
 
-def join(mine, theirs, scalars):
-    slots = len(mine)
-    rows, features = mine[0].shape
+def join(parts, scalars):
+    half, rows, features = parts[0].shape
     order = feature_order(features).T
     vmem = pl.BlockSpec(memory_space=pltpu.VMEM)
     return pl.pallas_call(
-        partial(join_kernel, slots=slots),
-        out_shape=jax.ShapeDtypeStruct((2 * slots * rows, features), bf16),
-        in_specs=[pl.BlockSpec(memory_space=pltpu.SMEM)] + [vmem] * (slots + 2),
+        join_kernel,
+        out_shape=jax.ShapeDtypeStruct((4 * half * rows, features), bf16),
+        in_specs=[pl.BlockSpec(memory_space=pltpu.SMEM)] + [vmem] * 5,
         out_specs=vmem,
-        scratch_shapes=[pltpu.VMEM((2 * slots * rows, features), f32)],
+        scratch_shapes=[pltpu.VMEM((4 * half * rows, features), f32)],
         compiler_params=pltpu.CompilerParams(vmem_limit_bytes=20 * MIB),
         cost_estimate=pl.CostEstimate(flops=1_700_000_000, bytes_accessed=5_000_000, transcendentals=0),
         name="join",
-    )(scalars, *mine, theirs, order)
+    )(scalars, *parts, order)
 
 
 def tail_kernel(scalars, own_ref, far_ref, embed_ref, inverse_ref, plain_ref, *rest, slots):
@@ -394,18 +396,25 @@
     )
 
 
-def mlp_kernel(*refs, count):
+def mlp_kernel(scalars, *refs, picks, count):
+    held = sum(picks)
     w_refs, (normed_own, normed_far, cot_own, cot_far), outs = (
-        refs[:count],
-        refs[count : count + 4],
-        refs[count + 4 :],
+        list(refs[:held]),
+        refs[held : held + 4],
+        refs[held + 4 :],
     )
     act_own, act_far, w_out = outs[:3]
     grads = outs[3:]
-    hidden, model = w_refs[0].shape
-    tokens = normed_own.shape[1]
+    model, tokens = normed_own.shape
+    hidden = w_out.shape[0] // count
     for k in range(count):
-        w_out[pl.ds(k * hidden, hidden), :] = w_refs[k][...]
+        if picks[k] == 1:
+            w_out[pl.ds(k * hidden, hidden), :] = w_refs.pop(0)[...]
+            continue
+        mid = hidden // 2
+        for half in (scalars[3], 1 - scalars[3]):
+            at = pl.multiple_of(k * hidden + half * mid, mid)
+            w_out[pl.ds(at, mid), :] = w_refs.pop(0)[...]
     tile = min(tokens, 256)
     for normed, cot, act in ((normed_own, cot_own, act_own), (normed_far, cot_far, act_far)):
         for i in range(0, tokens, tile):
@@ -417,62 +426,73 @@
         cols = pl.ds(i, min(256, model - i))
         value = contract(act_own[...], normed_own[cols, :], 1, 1)
         value = (value + contract(act_far[...], normed_far[cols, :], 1, 1)).astype(bf16)
-        for k in range(count):
-            grads[k][:, cols] = value[k * hidden : (k + 1) * hidden]
-
-
-def mlp(w_slots, normed, cots, part):
+        rows = grads[0].shape[0]
+        for k in range(len(grads)):
+            grads[k][:, cols] = value[k * rows : (k + 1) * rows]
+
+
+def mlp(scalars, w_slots, normed, cots, pieces):
     count = len(w_slots)
-    hidden, model = w_slots[0].shape
+    picks = tuple(len(pieces) for pieces in w_slots)
+    w_pieces = [piece for pieces in w_slots for piece in pieces]
+    hidden, model = w_slots[0][0].shape
     tokens = normed[0].shape[1]
     vmem = pl.BlockSpec(memory_space=pltpu.VMEM)
-    cot_spec = pl.BlockSpec((count, hidden, tokens), lambda i: (part, 0, 0))
+    cot_spec = pl.BlockSpec((count, hidden, tokens), lambda i: (0, 0, 0))
     whole = pl.BlockSpec((model, tokens), lambda i: (0, 0))
-    slot = pl.BlockSpec((hidden, model), lambda i: (0, 0))
+    slot = pl.BlockSpec((hidden // pieces, model), lambda i: (0, 0))
     wide = pl.BlockSpec((count * hidden, tokens), lambda i: (0, 0))
     return pl.pallas_call(
-        partial(mlp_kernel, count=count),
+        partial(mlp_kernel, picks=picks, count=count),
         grid=(1,),
         out_shape=[jax.ShapeDtypeStruct((count * hidden, tokens), bf16)] * 2
         + [jax.ShapeDtypeStruct((count * hidden, model), bf16)]
-        + [jax.ShapeDtypeStruct((hidden, model), bf16)] * count,
-        in_specs=[slot] * count + [whole] * 2 + [cot_spec] * 2,
-        out_specs=[wide] * 2 + [pl.BlockSpec((count * hidden, model), lambda i: (0, 0))] + [slot] * count,
+        + [jax.ShapeDtypeStruct((hidden // pieces, model), bf16)] * (count * pieces),
+        in_specs=[pl.BlockSpec(memory_space=pltpu.SMEM)]
+        + [pl.BlockSpec(piece.shape, lambda i: (0, 0)) for piece in w_pieces]
+        + [whole] * 2
+        + [cot_spec] * 2,
+        out_specs=[wide] * 2 + [pl.BlockSpec((count * hidden, model), lambda i: (0, 0))] + [slot] * (count * pieces),
         compiler_params=pltpu.CompilerParams(vmem_limit_bytes=30 * MIB),
         cost_estimate=pl.CostEstimate(
             flops=8 * count * hidden * model * tokens, bytes_accessed=15_000_000, transcendentals=0
         ),
-    )(*w_slots, *normed, *cots)
+    )(scalars, *w_pieces, *normed, *cots)
 
 
 def bits_of(size):
     return [1 << i for i in range(size.bit_length() - 1)]
 
 
-def gather_slots(shard, axis, order):
-    slots = {0: shard}
+def gather_slots(slots, axis, order):
     for bit in order:
         for k in list(slots):
             slots[k ^ bit] = exchange(slots[k], axis, bit)
-    return [slots[k] for k in range(len(slots))]
-
-
-def near_slots(shard, axis):
-    slots = [shard]
-    for k in range(2, lax.axis_size(axis), 2):
-        slots += [None, exchange(shard, axis, k)]
-    pairs = [exchange(slot, axis, 1) for slot in slots[::2]]
-    return [slot for both in zip(slots[::2], pairs) for slot in both]
-
-
-def scatter_slots(slots, axis, order):
-    live = dict(enumerate(slots))
+    return [slots[k] for k in sorted(slots)]
+
+
+def reduce_slots(live, axis, order):
+    live = dict(live)
     for bit in order:
         for k in sorted(k for k in live if k & bit):
             arrived = exchange(live.pop(k), axis, bit)
-            total = live[k ^ bit].astype(f32) + arrived.astype(f32)
-            live[k ^ bit] = total if bit == order[-1] else total.astype(bf16)
-    return live[0]
+            live[k ^ bit] = (live[k ^ bit].astype(f32) + arrived.astype(f32)).astype(bf16)
+    (last,) = live.values()
+    return last
+
+
+def scatter_slots(slots, axis, bits):
+    half = len(slots) // 2
+    turned = bits[1::-1] + bits[2:-1] if len(slots[half]) > 1 else bits[:-1]
+    near = reduce_slots({k: slots[k] for k in range(half)}, axis, turned)
+    pieces = len(slots[half])
+    sums = []
+    for i in range(pieces):
+        far = reduce_slots({k: slots[k][i] for k in range(half, 2 * half)}, axis, bits[:-1])
+        arrived = exchange(far, axis, half)
+        rows = far.shape[0]
+        sums.append(near[i * rows : (i + 1) * rows].astype(f32) + arrived.astype(f32))
+    return jnp.concatenate(sums, axis=0) if pieces > 1 else sums[0]
 
 
 def swap(value):
@@ -486,8 +506,10 @@
     bits = bits_of(devs)
     me = lax.axis_index("dev")
     core = lax.axis_index("rve")
+    parity = lax.axis_index("groups") % 2
     features = w_embed.shape[1]
     rows_embed = w_embed.shape[0]
+    hidden = w_up.shape[0]
     tokens = cotangent.shape[0]
     bands_in = ny // devs // PATCH_Y
     grad_scale = 1.0 / math.sqrt(tokens * devs * 2)
@@ -498,16 +520,40 @@
     before = lax.ppermute(small[slab - SWEEPS :], "dev", up)
     after = lax.ppermute(small[:SWEEPS], "dev", down)
 
-    scalars = jnp.stack([me, core, load_case[0]]).astype(jnp.int32)
+    scalars = jnp.stack([me, core, load_case[0], parity]).astype(jnp.int32)
     outs = solve(phase, before, after, scalars, moduli, loading_table, devs)
     displace, blocks = (outs[0], outs[1:])
 
-    embed_slots = near_slots(w_embed, "dev")
-    w_all = join(embed_slots, swap(jnp.stack(embed_slots)), scalars)
-
-    up_slots = gather_slots(w_up, "dev", bits[::-1])
-    cot_own, cot_other = turn(cotangent, scalars, devs)
-    cots = (cot_own, swap(cot_other))
+    near = [w_embed] + [exchange(w_embed, "dev", k) for k in range(2, devs, 2)]
+    even = jnp.stack(near)
+    odd = exchange(even, "dev", 1)
+    w_all = join((even, odd, swap(even), swap(odd)), scalars)
+
+    mid = hidden // 2
+
+    def mine(value):
+        return lax.dynamic_slice_in_dim(value, parity * mid, mid, 0)
+
+    near = exchange(mine(w_up), "dev", devs // 2)
+    far = exchange(near, "groups", 1)
+    top = jnp.concatenate(
+        [jnp.where(parity == 0, near, far), jnp.where(parity == 0, far, near)], axis=0
+    )
+    up_even = gather_slots({0: w_up, devs // 2: top}, "dev", bits[-2:0:-1])
+    up_slots = []
+    for i, value in enumerate(up_even):
+        k = 2 * i + 1
+        if k in (1, devs - 1):
+            up_slots += [(value,), (exchange(value, "dev", 1),)]
+        else:
+            rows = mine(value)
+            near = exchange(rows, "dev", 1)
+            up_slots += [(value,), (near, exchange(near, "groups", 1))]
+
+    cots = []
+    for part in range(2):
+        cot_own, cot_other = turn(cotangent, scalars, devs, part)
+        cots.append((cot_own, swap(cot_other)))
 
     arrived = [blocks[0]] + [exchange(blocks[k], "dev", k) for k in range(1, devs)]
     patches, plain = patchify(arrived, scalars, bands_in)
@@ -516,12 +562,13 @@
     normed_far, _, _ = embed(w_all, far_patches)
 
     half = devs // 2
-    grads = [None] * devs
+    grads = []
     own_parts, far_parts, w_parts = ([], [], [])
-    for part in (1, 0):
-        act_own, act_far, w_part, *grads[part * half : (part + 1) * half] = mlp(
-            up_slots[part * half : (part + 1) * half], (normed_own, normed_far), cots, part
+    for part in range(2):
+        act_own, act_far, w_part, *outs = mlp(
+            scalars, up_slots[part * half : (part + 1) * half], (normed_own, normed_far), cots[part], 1 + part
         )
+        grads += [tuple(outs[2 * k : 2 * k + 2]) for k in range(half)] if part else outs
         own_parts.append(act_own)
         far_parts.append(act_far)
         w_parts.append(w_part)
@@ -533,7 +580,7 @@
     *mine, yours = tail(own_grad, partner, embedded, inverse_rms, plain, scalars, devs)
     arrived = swap(yours).reshape(devs, rows_embed, features)
     mine = [(m.astype(f32) + arrived[k].astype(f32)).astype(bf16) for k, m in enumerate(mine)]
-    grad_embed = scatter_slots(mine, "dev", bits[1::-1] + bits[2:]) * grad_scale
+    grad_embed = scatter_slots(mine[:half] + [(m,) for m in mine[half:]], "dev", bits) * grad_scale
     return (displace[None], grad_embed, grad_up)
 
 

time: 256 us -> 185 us (0.72)
  waiting for transfers between devices: 126 us -> 60.6 us
  starting transfers between devices: 64.4 us -> 59.5 us
  other arithmetic: 5.04 us -> 8.84 us
  Pallas kernels: 46 us -> 42.5 us
    ppermute x40 -> x46, waiting for transfers between devices: 126 us -> 60.6 us  [exchange(): return lax.ppermute(value, axis, [(i, i ^ bit) for i in range(size)])]
    pallas_call x1 -> x2, Pallas kernels: 7.49 us -> 3.2 us  [turn(): pl.pallas_call(turn_kernel, out_shape=[out, out], grid_spec=pltpu.Prefetc...]
    ppermute x40 -> x46, starting transfers between devices: 58.6 us -> 54.6 us  [exchange(): return lax.ppermute(value, axis, [(i, i ^ bit) for i in range(size)])]
  transfers between devices with their start and end apart: 42 -> 48, of which waited for: 17 -> 18; matrix products, arithmetic and copies ran while one was open for 6% -> 9% of each run, Pallas kernels for 16% -> 23%
where the time goes in v1:
time: 185 us
  waiting for transfers between devices  60.6 us (33%)
  starting transfers between devices  59.5 us (32%)
  Pallas kernels  42.5 us (23%)
  other arithmetic  8.84 us (5%)
  local copies, waits for them, and re-layouts  6.19 us (3%)
  matrix products  5.42 us (3%)
    ppermute x46, waiting for transfers between devices, exchange(): return lax.ppermute(value, axis, [(i, i ^ bit) for i in range(size)])  60.6 us
    ppermute x46, starting transfers between devices, exchange(): return lax.ppermute(value, axis, [(i, i ^ bit) for i in range(size)])  54.6 us
    pallas_call x2, Pallas kernels, mlp(): pl.pallas_call(partial(mlp_kernel, picks=picks, count=count), grid=(1,),...  13.6 us
    pallas_call x1, Pallas kernels, solve(): pl.pallas_call(partial(solver_kernel, slab=slab, bands=bands, patch_y=PAT...  12.8 us
    dot_general x4, matrix products, contract(): lax.dot_general(left, right, (((left_dim,), (right_dim,)), ((), ())), pre...  5.42 us
    pallas_call x2, Pallas kernels, embed(): pl.pallas_call(embed_kernel, out_shape=[jax.ShapeDtypeStruct((model, toke...  4.47 us
    unnamed x33, local copies, waits for them, and re-layouts  3.76 us
  transfers between devices with their start and end apart: 48, of which 18 were waited for; matrix products, arithmetic and copies ran while one was open for 9% of the time, Pallas kernels for 23%

profile of v1, /device:TPU:0, one launch (start us, length us, event | category | flops | bytes accessed | tf_op | source)
XLA Modules:
  0.0 184.8 jit_solution(6486984693310868050)
XLA Ops:
  0.7 3.1 %collective-permute-start.6 = (bf16[88,768]{1,0:T(8,128)(2,1)}, bf16[88,768]{1,0:T(8,128)(2,1)}, u32[]{:S(2)}, u32[]{:S(2)}) collective-permute-start(bf16[88,768]{1,0:T(8,128)(2,1)} %param.11), channel_id=1, source_target_pairs={{0,4},{2,6},{4,0},{6,2},{8,12},{10,14},{12,8},{14,10},{1,5},{3,7},... | collective-permute-start | bytes 405512 | tf_op jit(solution)/shard_map/ppermute | solution.py:31
  3.8 2.6 %collective-permute-start.7 = (bf16[88,768]{1,0:T(8,128)(2,1)}, bf16[88,768]{1,0:T(8,128)(2,1)}, u32[]{:S(2)}, u32[]{:S(2)}) collective-permute-start(bf16[88,768]{1,0:T(8,128)(2,1)} %param.11), channel_id=1, source_target_pairs={{0,8},{2,10},{4,12},{6,14},{8,0},{10,2},{12,4},{14,6},{1,9},{3,11}... | collective-permute-start | bytes 405512 | tf_op jit(solution)/shard_map/ppermute | solution.py:31
  8.2 3.7 %collective-permute-start = (bf16[4,128,128]{2,1,0:T(8,128)(2,1)}, bf16[4,128,128]{2,1,0:T(8,128)(2,1)S(1)}, u32[]{:S(2)}, u32[]{:S(2)}) collective-permute-start(bf16[4,128,128]{2,1,0:T(8,128)(2,1)} %get-tuple-element.106), channel_id=1, source_target_pairs={{0,2},{2,4},{4,6},{6,8},{8,10},{10,12},{12,14},{1,3},{3,5},{5,7},{... | collective-permute-start | bytes 393224 | tf_op jit(solution)/shard_map/ppermute | solution.py:520
  14.9 2.4 %collective-permute-start.21 = (bf16[96,1408]{1,0:T(8,128)(2,1)}, bf16[96,1408]{1,0:T(8,128)(2,1)}, u32[]{:S(2)}, u32[]{:S(2)}) collective-permute-start(bf16[96,1408]{1,0:T(8,128)(2,1)} %constant_dynamic-slice_fusion), channel_id=1, source_target_pairs={{0,8},{2,10},{4,12},{6,14},{8,0},{10,2},{12,4},{14,6},{1,9},{3,11}... | collective-permute-start | bytes 811016 | tf_op jit(solution)/shard_map/ppermute | solution.py:31
  19.4 2.5 %collective-permute-start.8 = (bf16[88,768]{1,0:T(8,128)(2,1)}, bf16[88,768]{1,0:T(8,128)(2,1)}, u32[]{:S(2)}, u32[]{:S(2)}) collective-permute-start(bf16[88,768]{1,0:T(8,128)(2,1)} %param.11), channel_id=1, source_target_pairs={{0,12},{2,14},{4,8},{6,10},{8,4},{10,6},{12,0},{14,2},{1,13},{3,15... | collective-permute-start | bytes 405512 | tf_op jit(solution)/shard_map/ppermute | solution.py:31
  23.0 12.8 %solver.1 = (f32[3,8,128,128]{3,2,1,0:T(8,128)}, bf16[384,128]{1,0:T(8,128)(2,1)S(1)}, bf16[384,128]{1,0:T(8,128)(2,1)}, bf16[384,128]{1,0:T(8,128)(2,1)}, bf16[...) custom-call(s32[4]{0:T(128)S(1)} %pad_add_fusion.scalars, ...), custom_call_target="tpu_custom_call" | custom-call | flops 40000000 | bytes 4000000 | tf_op jit(solution)/shard_map/solver/pallas_call | solution.py:174
  38.9 7.9 %collective-permute-start.13 = (bf16[384,128]{1,0:T(8,128)(2,1)}, bf16[384,128]{1,0:T(8,128)(2,1)}, u32[]{:S(2)}, u32[]{:S(2)}) collective-permute-start(bf16[384,128]{1,0:T(8,128)(2,1)} %get-tuple-element.52), channel_id=1, source_target_pairs={{0,4},{2,6},{4,0},{6,2},{8,12},{10,14},{12,8},{14,10},{1,5},{3,7},... | collective-permute-start | bytes 294920 | tf_op jit(solution)/shard_map/ppermute | solution.py:31
  51.9 2.9 %collective-permute-start.16 = (bf16[384,128]{1,0:T(8,128)(2,1)S(1)}, bf16[384,128]{1,0:T(8,128)(2,1)S(1)}, u32[]{:S(2)}, u32[]{:S(2)}) collective-permute-start(bf16[384,128]{1,0:T(8,128)(2,1)S(1)} %copy-done.11), channel_id=1, source_target_pairs={{0,10},{2,8},{4,14},{6,12},{8,2},{10,0},{12,6},{14,4},{1,11},{3,9}... | collective-permute-start | bytes 294920 | tf_op jit(solution)/shard_map/ppermute | solution.py:31
  56.3 2.3 %collective-permute-start.18 = (bf16[384,128]{1,0:T(8,128)(2,1)S(1)}, bf16[384,128]{1,0:T(8,128)(2,1)S(1)}, u32[]{:S(2)}, u32[]{:S(2)}) collective-permute-start(bf16[384,128]{1,0:T(8,128)(2,1)S(1)} %copy-done.7), channel_id=1, source_target_pairs={{0,14},{2,12},{4,10},{6,8},{8,6},{10,4},{12,2},{14,0},{1,15},{3,13... | collective-permute-start | bytes 294920 | tf_op jit(solution)/shard_map/ppermute | solution.py:31
  64.5 2.3 %patchify.1 = (bf16[768,512]{1,0:T(8,128)(2,1)S(1)}, bf16[768,512]{1,0:T(8,128)(2,1)S(1)}) custom-call(s32[4]{0:T(128)S(1)} %pad_add_fusion.scalars, bf16[384,128]{1,0:T(8,128)(2,1)S(1)} %get-tuple-element.50.refs_0_, bf16[384,128]{1,0:T(8,128)(2,1)S(1)} %collective-permute-done.12.refs_1_, bf16[384,128]{1,0:T(8,128)(2,1)} %collective-permute-done.13.refs_2_, ...), custom_call_target="tpu_custom_call" | custom-call | flops 1000000000 | bytes 5000000 | tf_op jit(solution)/shard_map/patchify/pallas_call | solution.py:235
  69.9 4.5 %collective-permute-done.2.refs_1_ = bf16[192,1408]{1,0:T(8,128)(2,1)S(1)} collective-permute-done((bf16[192,1408]{1,0:T(8,128)(2,1)S(1)}, bf16[192,1408]{1,0:T(8,128)(2,1)S(1)}, u32[]{:S(2)}, u32[]{:S(2)}) %collective-permute-start.2) | collective-permute-done | bytes 540704 | tf_op jit(solution)/shard_map/ppermute | solution.py:31
  75.2 9.0 %collective-permute-done.9.odd = bf16[4,88,768]{2,1,0:T(8,128)(2,1)S(1)} collective-permute-done((bf16[4,88,768]{2,1,0:T(8,128)(2,1)S(1)}, bf16[4,88,768]{2,1,0:T(8,128)(2,1)S(1)}, u32[]{:S(2)}, u32[]{:S(2)}) %collective-permute-start.9) | collective-permute-done | bytes 540704 | tf_op jit(solution)/shard_map/ppermute | solution.py:31
  90.1 2.7 %join.1.w_ref = bf16[1408,768]{1,0:T(8,128)(2,1)S(1)} custom-call(s32[4]{0:T(128)S(1)} %pad_add_fusion.scalars, bf16[4,88,768]{2,1,0:T(8,128)(2,1)S(1)} %pad_maximum_fusion.1.even, bf16[4,88,768]{2,1,0:T(8,128)(2,1)S(1)} %collective-permute-done.9.odd, bf16[4,88,768]{2,1,0:T(8,128)(2,1)S(1)} %collective-permute-done.10.even_far, ...), custom_call_target="tpu_custom_call" | custom-call | flops 1700000000 | bytes 5000000 | tf_op jit(solution)/shard_map/join/pallas_call | solution.py:334
  92.8 6.5 %collective-permute-done.25.refs_3_ = bf16[192,1408]{1,0:T(8,128)(2,1)S(1)} collective-permute-done((bf16[192,1408]{1,0:T(8,128)(2,1)S(1)}, bf16[192,1408]{1,0:T(8,128)(2,1)S(1)}, u32[]{:S(2)}, u32[]{:S(2)}) %collective-permute-start.25) | collective-permute-done | bytes 540704 | tf_op jit(solution)/shard_map/ppermute | solution.py:31
  102.0 2.7 %embed.3 = (bf16[1408,512]{1,0:T(8,128)(2,1)S(1)}, bf16[1408,512]{1,0:T(8,128)(2,1)}, f32[1,512]{1,0:T(1,128)}) custom-call(bf16[1408,768]{1,0:T(8,128)(2,1)S(1)} %join.1.w_ref, bf16[768,512]{1,0:T(8,128)(2,1)S(1)} %collective-permute-done.19.patch_ref), custom_call_target="tpu_custom_call" | custom-call | flops 1107296256 | bytes 6000000 | tf_op jit(solution)/shard_map/embed/pallas_call | solution.py:302
  106.2 6.7 %shard_map.95 = (bf16[768,512]{1,0:T(8,128)(2,1)S(1)}, bf16[768,512]{1,0:T(8,128)(2,1)S(1)}, bf16[768,1408]{1,0:T(8,128)(2,1)S(1)}, bf16[192,1408]{1,0:T(8,128)(...) custom-call(s32[4]{0:T(128)S(1)} %pad_add_fusion.scalars, ...), custom_call_target="tpu_custom_call" | custom-call | flops 4429185024 | bytes 15000000 | tf_op jit(solution)/shard_map/pallas_call | solution.py:445
  115.1 6.9 %shard_map.97 = (bf16[768,512]{1,0:T(8,128)(2,1)S(1)}, bf16[768,512]{1,0:T(8,128)(2,1)S(1)}, bf16[768,1408]{1,0:T(8,128)(2,1)S(1)}, bf16[96,1408]{1,0:T(8,128)(2...) custom-call(s32[4]{0:T(128)S(1)} %pad_add_fusion.scalars, ...), custom_call_target="tpu_custom_call" | custom-call | flops 4429185024 | bytes 15000000 | tf_op jit(solution)/shard_map/pallas_call | solution.py:445
  133.7 3.4 %tail.1 = (bf16[88,768]{1,0:T(8,128)(2,1)S(1)}, bf16[88,768]{1,0:T(8,128)(2,1)S(1)}, bf16[88,768]{1,0:T(8,128)(2,1)S(1)}, bf16[88,768]{1,0:T(8,128)(2,1)S(1)}, b...) custom-call(s32[4]{0:T(128)S(1)} %pad_add_fusion.scalars, ...), custom_call_target="tpu_custom_call" | custom-call | flops 1200000000 | bytes 9000000 | tf_op jit(solution)/shard_map/tail/pallas_call | solution.py:377
  137.0 5.5 %collective-permute-done.41 = bf16[96,1408]{1,0:T(8,128)(2,1)S(1)} collective-permute-done((bf16[96,1408]{1,0:T(8,128)(2,1)S(1)}, bf16[96,1408]{1,0:T(8,128)(2,1)S(1)}, u32[]{:S(2)}, u32[]{:S(2)}) %collective-permute-start.41) | collective-permute-done | bytes 270368 | tf_op jit(solution)/shard_map/ppermute | solution.py:31
  148.4 9.4 %collective-permute-done.42 = bf16[96,1408]{1,0:T(8,128)(2,1)S(1)} collective-permute-done((bf16[96,1408]{1,0:T(8,128)(2,1)S(1)}, bf16[96,1408]{1,0:T(8,128)(2,1)S(1)}, u32[]{:S(2)}, u32[]{:S(2)}) %collective-permute-start.42) | collective-permute-done | bytes 270368 | tf_op jit(solution)/shard_map/ppermute | solution.py:31
  161.4 3.3 %collective-permute-done.31 = bf16[88,768]{1,0:T(8,128)(2,1)S(1)} collective-permute-done((bf16[88,768]{1,0:T(8,128)(2,1)S(1)}, bf16[88,768]{1,0:T(8,128)(2,1)S(1)}, u32[]{:S(2)}, u32[]{:S(2)}) %collective-permute-start.31) | collective-permute-done | bytes 135200 | tf_op jit(solution)/shard_map/ppermute | solution.py:31
  164.7 2.6 %collective-permute-done.34 = bf16[88,768]{1,0:T(8,128)(2,1)S(1)} collective-permute-done((bf16[88,768]{1,0:T(8,128)(2,1)S(1)}, bf16[88,768]{1,0:T(8,128)(2,1)S(1)}, u32[]{:S(2)}, u32[]{:S(2)}) %collective-permute-start.34) | collective-permute-done | bytes 135200 | tf_op jit(solution)/shard_map/ppermute | solution.py:31
  168.7 3.0 %collective-permute-done.43 = bf16[96,1408]{1,0:T(8,128)(2,1)S(1)} collective-permute-done((bf16[96,1408]{1,0:T(8,128)(2,1)S(1)}, bf16[96,1408]{1,0:T(8,128)(2,1)S(1)}, u32[]{:S(2)}, u32[]{:S(2)}) %collective-permute-start.43) | collective-permute-done | bytes 270368 | tf_op jit(solution)/shard_map/ppermute | solution.py:31
  177.8 6.2 %collective-permute-done.36 = bf16[88,768]{1,0:T(8,128)(2,1)S(1)} collective-permute-done((bf16[88,768]{1,0:T(8,128)(2,1)S(1)}, bf16[88,768]{1,0:T(8,128)(2,1)S(1)}, u32[]{:S(2)}, u32[]{:S(2)}) %collective-permute-start.36) | collective-permute-done | bytes 135200 | tf_op jit(solution)/shard_map/ppermute | solution.py:31
  (144 shorter events, 68.1 us)
Async XLA Ops:
  0.7 38.3 %collective-permute-start.6 = (bf16[88,768]{1,0:T(8,128)(2,1)}, bf16[88,768]{1,0:T(8,128)(2,1)}, u32[]{:S(2)}, u32[]{:S(2)}) collective-permute-start(bf16[88,768]{1,0:T(8,128)(2,1)} %param.11), channel_id=1, source_target_pairs={{0,4},{2,6},{4,0},{6,2},{8,12},{10,14},{12,8},{14,10},{1,5},{3,7},... | collective-permute-start | bytes 405512 | tf_op jit(solution)/shard_map/ppermute | solution.py:31
  3.8 43.1 %collective-permute-start.7 = (bf16[88,768]{1,0:T(8,128)(2,1)}, bf16[88,768]{1,0:T(8,128)(2,1)}, u32[]{:S(2)}, u32[]{:S(2)}) collective-permute-start(bf16[88,768]{1,0:T(8,128)(2,1)} %param.11), channel_id=1, source_target_pairs={{0,8},{2,10},{4,12},{6,14},{8,0},{10,2},{12,4},{14,6},{1,9},{3,11}... | collective-permute-start | bytes 405512 | tf_op jit(solution)/shard_map/ppermute | solution.py:31
  14.9 32.0 %collective-permute-start.21 = (bf16[96,1408]{1,0:T(8,128)(2,1)}, bf16[96,1408]{1,0:T(8,128)(2,1)}, u32[]{:S(2)}, u32[]{:S(2)}) collective-permute-start(bf16[96,1408]{1,0:T(8,128)(2,1)} %constant_dynamic-slice_fusion), channel_id=1, source_target_pairs={{0,8},{2,10},{4,12},{6,14},{8,0},{10,2},{12,4},{14,6},{1,9},{3,11}... | collective-permute-start | bytes 811016 | tf_op jit(solution)/shard_map/ppermute | solution.py:31
  19.4 31.6 %collective-permute-start.8 = (bf16[88,768]{1,0:T(8,128)(2,1)}, bf16[88,768]{1,0:T(8,128)(2,1)}, u32[]{:S(2)}, u32[]{:S(2)}) collective-permute-start(bf16[88,768]{1,0:T(8,128)(2,1)} %param.11), channel_id=1, source_target_pairs={{0,12},{2,14},{4,8},{6,10},{8,4},{10,6},{12,0},{14,2},{1,13},{3,15... | collective-permute-start | bytes 405512 | tf_op jit(solution)/shard_map/ppermute | solution.py:31
  38.9 15.9 %collective-permute-start.13 = (bf16[384,128]{1,0:T(8,128)(2,1)}, bf16[384,128]{1,0:T(8,128)(2,1)}, u32[]{:S(2)}, u32[]{:S(2)}) collective-permute-start(bf16[384,128]{1,0:T(8,128)(2,1)} %get-tuple-element.52), channel_id=1, source_target_pairs={{0,4},{2,6},{4,0},{6,2},{8,12},{10,14},{12,8},{14,10},{1,5},{3,7},... | collective-permute-start | bytes 294920 | tf_op jit(solution)/shard_map/ppermute | solution.py:31
  46.8 20.0 %collective-permute-start.22 = (bf16[96,1408]{1,0:T(8,128)(2,1)}, bf16[96,1408]{1,0:T(8,128)(2,1)}, u32[]{:S(2)}, u32[]{:S(2)}) collective-permute-start(bf16[96,1408]{1,0:T(8,128)(2,1)} %collective-permute-done.21), channel_id=1, source_target_pairs={{0,16},{16,0},{1,17},{17,1},{2,18},{18,2},{3,19},{19,3},{4,20},{20... | collective-permute-start | bytes 811016 | tf_op jit(solution)/shard_map/ppermute | solution.py:31
  59.9 14.5 %collective-permute-start.2 = (bf16[192,1408]{1,0:T(8,128)(2,1)S(1)}, bf16[192,1408]{1,0:T(8,128)(2,1)S(1)}, u32[]{:S(2)}, u32[]{:S(2)}) collective-permute-start(bf16[192,1408]{1,0:T(8,128)(2,1)S(1)} %copy-done.4), channel_id=1, source_target_pairs={{0,2},{2,0},{4,6},{6,4},{8,10},{10,8},{12,14},{14,12},{1,3},{3,1},... | collective-permute-start | bytes 1622024 | tf_op jit(solution)/shard_map/ppermute | solution.py:31
  62.0 44.3 %collective-permute-start.20 = (bf16[4,192,512]{2,1,0:T(8,128)(2,1)S(1)}, bf16[4,192,512]{2,1,0:T(8,128)(2,1)S(1)}, u32[]{:S(2)}, u32[]{:S(2)}) collective-permute-start(bf16[4,192,512]{2,1,0:T(8,128)(2,1)S(1)} %get-tuple-element.62), channel_id=1, source_target_pairs={{0,1},{1,0},{2,3},{3,2},{4,5},{5,4},{6,7},{7,6},{8,9},{9,8},{10,11... | collective-permute-start | bytes 2359304 | tf_op jit(solution)/shard_map/ppermute | solution.py:31
  64.0 20.2 %collective-permute-start.9 = (bf16[4,88,768]{2,1,0:T(8,128)(2,1)S(1)}, bf16[4,88,768]{2,1,0:T(8,128)(2,1)S(1)}, u32[]{:S(2)}, u32[]{:S(2)}) collective-permute-start(bf16[4,88,768]{2,1,0:T(8,128)(2,1)S(1)} %pad_maximum_fusion.1.even), channel_id=1, source_target_pairs={{0,2},{2,0},{4,6},{6,4},{8,10},{10,8},{12,14},{14,12},{1,3},{3,1},... | collective-permute-start | bytes 1622024 | tf_op jit(solution)/shard_map/ppermute | solution.py:31
  66.8 17.4 %collective-permute-start.10 = (bf16[4,88,768]{2,1,0:T(8,128)(2,1)S(1)}, bf16[4,88,768]{2,1,0:T(8,128)(2,1)S(1)}, u32[]{:S(2)}, u32[]{:S(2)}) collective-permute-start(bf16[4,88,768]{2,1,0:T(8,128)(2,1)S(1)} %pad_maximum_fusion.1.even), channel_id=1, source_target_pairs={{0,1},{1,0},{2,3},{3,2},{4,5},{5,4},{6,7},{7,6},{8,9},{9,8},{10,11... | collective-permute-start | bytes 1622024 | tf_op jit(solution)/shard_map/ppermute | solution.py:31
  69.9 18.5 %collective-permute-start.19 = (bf16[768,512]{1,0:T(8,128)(2,1)S(1)}, bf16[768,512]{1,0:T(8,128)(2,1)S(1)}, u32[]{:S(2)}, u32[]{:S(2)}) collective-permute-start(bf16[768,512]{1,0:T(8,128)(2,1)S(1)} %get-tuple-element.58.patch_ref), channel_id=1, source_target_pairs={{0,1},{1,0},{2,3},{3,2},{4,5},{5,4},{6,7},{7,6},{8,9},{9,8},{10,11... | collective-permute-start | bytes 2359304 | tf_op jit(solution)/shard_map/ppermute | solution.py:31
  84.3 15.0 %collective-permute-start.25 = (bf16[192,1408]{1,0:T(8,128)(2,1)S(1)}, bf16[192,1408]{1,0:T(8,128)(2,1)S(1)}, u32[]{:S(2)}, u32[]{:S(2)}) collective-permute-start(bf16[192,1408]{1,0:T(8,128)(2,1)S(1)} %pad_maximum_fusion.refs_0_), channel_id=1, source_target_pairs={{0,4},{2,6},{4,0},{6,2},{8,12},{10,14},{12,8},{14,10},{1,5},{3,7},... | collective-permute-start | bytes 1622024 | tf_op jit(solution)/shard_map/ppermute | solution.py:31
  88.0 27.1 %collective-permute-start.27 = (bf16[4,192,512]{2,1,0:T(8,128)(2,1)S(1)}, bf16[4,192,512]{2,1,0:T(8,128)(2,1)S(1)}, u32[]{:S(2)}, u32[]{:S(2)}) collective-permute-start(bf16[4,192,512]{2,1,0:T(8,128)(2,1)S(1)} %get-tuple-element.66), channel_id=1, source_target_pairs={{0,1},{1,0},{2,3},{3,2},{4,5},{5,4},{6,7},{7,6},{8,9},{9,8},{10,11... | collective-permute-start | bytes 2359304 | tf_op jit(solution)/shard_map/ppermute | solution.py:31
  88.5 16.3 %collective-permute-start.23 = (bf16[96,1408]{1,0:T(8,128)(2,1)S(1)}, bf16[96,1408]{1,0:T(8,128)(2,1)S(1)}, u32[]{:S(2)}, u32[]{:S(2)}) collective-permute-start(bf16[96,1408]{1,0:T(8,128)(2,1)S(1)} %fusion.3), channel_id=1, source_target_pairs={{0,2},{2,0},{4,6},{6,4},{8,10},{10,8},{12,14},{14,12},{1,3},{3,1},... | collective-permute-start | bytes 811016 | tf_op jit(solution)/shard_map/ppermute | solution.py:31
  89.6 16.7 %collective-permute-start.5 = (bf16[96,1408]{1,0:T(8,128)(2,1)S(1)}, bf16[96,1408]{1,0:T(8,128)(2,1)S(1)}, u32[]{:S(2)}, u32[]{:S(2)}) collective-permute-start(bf16[96,1408]{1,0:T(8,128)(2,1)S(1)} %collective-permute-done.4.refs_3_), channel_id=1, source_target_pairs={{0,16},{16,0},{1,17},{17,1},{2,18},{18,2},{3,19},{19,3},{4,20},{20... | collective-permute-start | bytes 811016 | tf_op jit(solution)/shard_map/ppermute | solution.py:31
  99.2 15.8 %collective-permute-start.26 = (bf16[192,1408]{1,0:T(8,128)(2,1)S(1)}, bf16[192,1408]{1,0:T(8,128)(2,1)S(1)}, u32[]{:S(2)}, u32[]{:S(2)}) collective-permute-start(bf16[192,1408]{1,0:T(8,128)(2,1)S(1)} %collective-permute-done.25.refs_3_), channel_id=1, source_target_pairs={{0,2},{2,0},{4,6},{6,4},{8,10},{10,8},{12,14},{14,12},{1,3},{3,1},... | collective-permute-start | bytes 1622024 | tf_op jit(solution)/shard_map/ppermute | solution.py:31
  113.0 16.6 %collective-permute-start.38 = (bf16[192,1408]{1,0:T(8,128)(2,1)S(1)}, bf16[192,1408]{1,0:T(8,128)(2,1)S(1)}, u32[]{:S(2)}, u32[]{:S(2)}) collective-permute-start(bf16[192,1408]{1,0:T(8,128)(2,1)S(1)} %get-tuple-element.86), channel_id=1, source_target_pairs={{0,4},{2,6},{4,0},{6,2},{8,12},{10,14},{12,8},{14,10},{1,5},{3,7},... | collective-permute-start | bytes 1622024 | tf_op jit(solution)/shard_map/ppermute | solution.py:31
  113.8 45.2 %collective-permute-start.37 = (bf16[192,1408]{1,0:T(8,128)(2,1)S(1)}, bf16[192,1408]{1,0:T(8,128)(2,1)S(1)}, u32[]{:S(2)}, u32[]{:S(2)}) collective-permute-start(bf16[192,1408]{1,0:T(8,128)(2,1)S(1)} %get-tuple-element.84), channel_id=1, source_target_pairs={{0,4},{2,6},{4,0},{6,2},{8,12},{10,14},{12,8},{14,10},{1,5},{3,7},... | collective-permute-start | bytes 1622024 | tf_op jit(solution)/shard_map/ppermute | solution.py:31
  122.4 20.2 %collective-permute-start.44 = (bf16[96,1408]{1,0:T(8,128)(2,1)S(1)}, bf16[96,1408]{1,0:T(8,128)(2,1)S(1)}, u32[]{:S(2)}, u32[]{:S(2)}) collective-permute-start(bf16[96,1408]{1,0:T(8,128)(2,1)S(1)} %get-tuple-element.92), channel_id=1, source_target_pairs={{0,2},{2,0},{4,6},{6,4},{8,10},{10,8},{12,14},{14,12},{1,3},{3,1},... | collective-permute-start | bytes 811016 | tf_op jit(solution)/shard_map/ppermute | solution.py:31
  131.4 15.5 %collective-permute-start.40 = (bf16[96,1408]{1,0:T(8,128)(2,1)S(1)}, bf16[96,1408]{1,0:T(8,128)(2,1)S(1)}, u32[]{:S(2)}, u32[]{:S(2)}) collective-permute-start(bf16[96,1408]{1,0:T(8,128)(2,1)S(1)} %get-tuple-element.88), channel_id=1, source_target_pairs={{0,2},{2,0},{4,6},{6,4},{8,10},{10,8},{12,14},{14,12},{1,3},{3,1},... | collective-permute-start | bytes 811016 | tf_op jit(solution)/shard_map/ppermute | solution.py:31
  142.5 15.5 %collective-permute-start.29 = (bf16[704,768]{1,0:T(8,128)(2,1)S(1)}, bf16[704,768]{1,0:T(8,128)(2,1)S(1)}, u32[]{:S(2)}, u32[]{:S(2)}) collective-permute-start(bf16[704,768]{1,0:T(8,128)(2,1)S(1)} %get-tuple-element.75), channel_id=1, source_target_pairs={{0,1},{1,0},{2,3},{3,2},{4,5},{5,4},{6,7},{7,6},{8,9},{9,8},{10,11... | collective-permute-start | bytes 3244040 | tf_op jit(solution)/shard_map/ppermute | solution.py:31
  142.6 17.6 %collective-permute-start.39 = (bf16[192,1408]{1,0:T(8,128)(2,1)S(1)}, bf16[192,1408]{1,0:T(8,128)(2,1)S(1)}, u32[]{:S(2)}, u32[]{:S(2)}) collective-permute-start(bf16[192,1408]{1,0:T(8,128)(2,1)S(1)} %add_convert_fusion.1), channel_id=1, source_target_pairs={{0,2},{2,0},{4,6},{6,4},{8,10},{10,8},{12,14},{14,12},{1,3},{3,1},... | collective-permute-start | bytes 1622024 | tf_op jit(solution)/shard_map/ppermute | solution.py:31
  143.7 14.1 %collective-permute-start.42 = (bf16[96,1408]{1,0:T(8,128)(2,1)S(1)}, bf16[96,1408]{1,0:T(8,128)(2,1)S(1)}, u32[]{:S(2)}, u32[]{:S(2)}) collective-permute-start(bf16[96,1408]{1,0:T(8,128)(2,1)S(1)} %add_convert_fusion.7), channel_id=1, source_target_pairs={{0,4},{2,6},{4,0},{6,2},{8,12},{10,14},{12,8},{14,10},{1,5},{3,7},... | collective-permute-start | bytes 811016 | tf_op jit(solution)/shard_map/ppermute | solution.py:31
  146.9 21.8 %collective-permute-start.47 = (bf16[96,1408]{1,0:T(8,128)(2,1)S(1)}, bf16[96,1408]{1,0:T(8,128)(2,1)S(1)}, u32[]{:S(2)}, u32[]{:S(2)}) collective-permute-start(bf16[96,1408]{1,0:T(8,128)(2,1)S(1)} %add_convert_fusion.3), channel_id=1, source_target_pairs={{0,8},{2,10},{4,12},{6,14},{8,0},{10,2},{12,4},{14,6},{1,9},{3,11}... | collective-permute-start | bytes 811016 | tf_op jit(solution)/shard_map/ppermute | solution.py:31
  (40 other events, 373.7 us)

commit v2 on v1

--- a/solution.py
+++ b/solution.py
@@ -94,7 +94,10 @@
 
     def setup(row, carry):
         here = key[row]
-        own = faces(here, here)
+        own = [jnp.broadcast_to(values[kind, 0, 0], here.shape) for kind in range(2)]
+        for p in range(1, phases):
+            hit = here == (1 << p)
+            own = [jnp.where(hit, values[kind, p, p], own[kind]) for kind in range(2)]
         above_y = jnp.where(iota_y == ny - 1, here, shifted(here, 0, -1))
         above_z = jnp.where(iota_z == nz - 1, here, shifted(here, 1, -1))
         upper_y = faces(here, above_y)
@@ -120,7 +123,7 @@
             even[c, row] = forcing * inverse
         return carry
 
-    lax.fori_loop(1, total - 1, setup, 0)
+    lax.fori_loop(1, total - 1, setup, 0, unroll=2)
 
     buffers = (even, odd)
     for step in range(1, SWEEPS):
@@ -147,7 +150,7 @@
                     displace_ref[c, row - halo] = value
             return carry
 
-        lax.fori_loop(1 + step, total - 1 - step, sweep, 0)
+        lax.fori_loop(1 + step, total - 1 - step, sweep, 0, unroll=2)
 
     band_rows = ny // bands
     for k in range(bands):

time: 185 us -> 183 us (0.989)
  transfers between devices with their start and end apart: 48 -> 48, of which waited for: 18 -> 18; matrix products, arithmetic and copies ran while one was open for 9% -> 9% of each run, Pallas kernels for 23% -> 22%
where the time goes in v2:
time: 183 us
  waiting for transfers between devices  60.5 us (33%)
  starting transfers between devices  59.6 us (33%)
  Pallas kernels  40.7 us (22%)
  other arithmetic  8.84 us (5%)
  local copies, waits for them, and re-layouts  6.19 us (3%)
  matrix products  5.42 us (3%)
    ppermute x46, waiting for transfers between devices, exchange(): return lax.ppermute(value, axis, [(i, i ^ bit) for i in range(size)])  60.5 us
    ppermute x46, starting transfers between devices, exchange(): return lax.ppermute(value, axis, [(i, i ^ bit) for i in range(size)])  54.7 us
    pallas_call x2, Pallas kernels, mlp(): pl.pallas_call(partial(mlp_kernel, picks=picks, count=count), grid=(1,),...  13.6 us
    pallas_call x1, Pallas kernels, solve(): pl.pallas_call(partial(solver_kernel, slab=slab, bands=bands, patch_y=PAT...  11 us
    dot_general x4, matrix products, contract(): lax.dot_general(left, right, (((left_dim,), (right_dim,)), ((), ())), pre...  5.42 us
    pallas_call x2, Pallas kernels, embed(): pl.pallas_call(embed_kernel, out_shape=[jax.ShapeDtypeStruct((model, toke...  4.47 us
    unnamed x33, local copies, waits for them, and re-layouts  3.76 us
    ppermute x1, starting transfers between devices, local(): before = lax.ppermute(small[slab - SWEEPS:], 'dev', up)  3.68 us
  transfers between devices with their start and end apart: 48, of which 18 were waited for; matrix products, arithmetic and copies ran while one was open for 9% of the time, Pallas kernels for 22%

profile of v2, /device:TPU:0, one launch (start us, length us, event | category | flops | bytes accessed | tf_op | source)
XLA Modules:
  0.0 183.0 jit_solution(9917159377725441070)
XLA Ops:
  0.7 3.1 %collective-permute-start.6 = (bf16[88,768]{1,0:T(8,128)(2,1)}, bf16[88,768]{1,0:T(8,128)(2,1)}, u32[]{:S(2)}, u32[]{:S(2)}) collective-permute-start(bf16[88,768]{1,0:T(8,128)(2,1)} %param.11), channel_id=1, source_target_pairs={{0,4},{2,6},{4,0},{6,2},{8,12},{10,14},{12,8},{14,10},{1,5},{3,7},... | collective-permute-start | bytes 405512 | tf_op jit(solution)/shard_map/ppermute | solution.py:31
  3.8 2.6 %collective-permute-start.7 = (bf16[88,768]{1,0:T(8,128)(2,1)}, bf16[88,768]{1,0:T(8,128)(2,1)}, u32[]{:S(2)}, u32[]{:S(2)}) collective-permute-start(bf16[88,768]{1,0:T(8,128)(2,1)} %param.11), channel_id=1, source_target_pairs={{0,8},{2,10},{4,12},{6,14},{8,0},{10,2},{12,4},{14,6},{1,9},{3,11}... | collective-permute-start | bytes 405512 | tf_op jit(solution)/shard_map/ppermute | solution.py:31
  8.2 3.7 %collective-permute-start = (bf16[4,128,128]{2,1,0:T(8,128)(2,1)}, bf16[4,128,128]{2,1,0:T(8,128)(2,1)S(1)}, u32[]{:S(2)}, u32[]{:S(2)}) collective-permute-start(bf16[4,128,128]{2,1,0:T(8,128)(2,1)} %get-tuple-element.106), channel_id=1, source_target_pairs={{0,2},{2,4},{4,6},{6,8},{8,10},{10,12},{12,14},{1,3},{3,5},{5,7},{... | collective-permute-start | bytes 393224 | tf_op jit(solution)/shard_map/ppermute | solution.py:523
  14.9 2.4 %collective-permute-start.21 = (bf16[96,1408]{1,0:T(8,128)(2,1)}, bf16[96,1408]{1,0:T(8,128)(2,1)}, u32[]{:S(2)}, u32[]{:S(2)}) collective-permute-start(bf16[96,1408]{1,0:T(8,128)(2,1)} %constant_dynamic-slice_fusion), channel_id=1, source_target_pairs={{0,8},{2,10},{4,12},{6,14},{8,0},{10,2},{12,4},{14,6},{1,9},{3,11}... | collective-permute-start | bytes 811016 | tf_op jit(solution)/shard_map/ppermute | solution.py:31
  19.4 2.5 %collective-permute-start.8 = (bf16[88,768]{1,0:T(8,128)(2,1)}, bf16[88,768]{1,0:T(8,128)(2,1)}, u32[]{:S(2)}, u32[]{:S(2)}) collective-permute-start(bf16[88,768]{1,0:T(8,128)(2,1)} %param.11), channel_id=1, source_target_pairs={{0,12},{2,14},{4,8},{6,10},{8,4},{10,6},{12,0},{14,2},{1,13},{3,15... | collective-permute-start | bytes 405512 | tf_op jit(solution)/shard_map/ppermute | solution.py:31
  23.0 11.0 %solver.1 = (f32[3,8,128,128]{3,2,1,0:T(8,128)}, bf16[384,128]{1,0:T(8,128)(2,1)S(1)}, bf16[384,128]{1,0:T(8,128)(2,1)}, bf16[384,128]{1,0:T(8,128)(2,1)}, bf16[...) custom-call(s32[4]{0:T(128)S(1)} %pad_add_fusion.scalars, ...), custom_call_target="tpu_custom_call" | custom-call | flops 40000000 | bytes 4000000 | tf_op jit(solution)/shard_map/solver/pallas_call | solution.py:177
  37.2 7.9 %collective-permute-start.13 = (bf16[384,128]{1,0:T(8,128)(2,1)}, bf16[384,128]{1,0:T(8,128)(2,1)}, u32[]{:S(2)}, u32[]{:S(2)}) collective-permute-start(bf16[384,128]{1,0:T(8,128)(2,1)} %get-tuple-element.52), channel_id=1, source_target_pairs={{0,4},{2,6},{4,0},{6,2},{8,12},{10,14},{12,8},{14,10},{1,5},{3,7},... | collective-permute-start | bytes 294920 | tf_op jit(solution)/shard_map/ppermute | solution.py:31
  50.2 2.9 %collective-permute-start.16 = (bf16[384,128]{1,0:T(8,128)(2,1)S(1)}, bf16[384,128]{1,0:T(8,128)(2,1)S(1)}, u32[]{:S(2)}, u32[]{:S(2)}) collective-permute-start(bf16[384,128]{1,0:T(8,128)(2,1)S(1)} %copy-done.11), channel_id=1, source_target_pairs={{0,10},{2,8},{4,14},{6,12},{8,2},{10,0},{12,6},{14,4},{1,11},{3,9}... | collective-permute-start | bytes 294920 | tf_op jit(solution)/shard_map/ppermute | solution.py:31
  54.6 2.3 %collective-permute-start.18 = (bf16[384,128]{1,0:T(8,128)(2,1)S(1)}, bf16[384,128]{1,0:T(8,128)(2,1)S(1)}, u32[]{:S(2)}, u32[]{:S(2)}) collective-permute-start(bf16[384,128]{1,0:T(8,128)(2,1)S(1)} %copy-done.7), channel_id=1, source_target_pairs={{0,14},{2,12},{4,10},{6,8},{8,6},{10,4},{12,2},{14,0},{1,15},{3,13... | collective-permute-start | bytes 294920 | tf_op jit(solution)/shard_map/ppermute | solution.py:31
  62.7 2.3 %patchify.1 = (bf16[768,512]{1,0:T(8,128)(2,1)S(1)}, bf16[768,512]{1,0:T(8,128)(2,1)S(1)}) custom-call(s32[4]{0:T(128)S(1)} %pad_add_fusion.scalars, bf16[384,128]{1,0:T(8,128)(2,1)S(1)} %get-tuple-element.50.refs_0_, bf16[384,128]{1,0:T(8,128)(2,1)S(1)} %collective-permute-done.12.refs_1_, bf16[384,128]{1,0:T(8,128)(2,1)} %collective-permute-done.13.refs_2_, ...), custom_call_target="tpu_custom_call" | custom-call | flops 1000000000 | bytes 5000000 | tf_op jit(solution)/shard_map/patchify/pallas_call | solution.py:238
  68.2 4.5 %collective-permute-done.2.refs_1_ = bf16[192,1408]{1,0:T(8,128)(2,1)S(1)} collective-permute-done((bf16[192,1408]{1,0:T(8,128)(2,1)S(1)}, bf16[192,1408]{1,0:T(8,128)(2,1)S(1)}, u32[]{:S(2)}, u32[]{:S(2)}) %collective-permute-start.2) | collective-permute-done | bytes 540704 | tf_op jit(solution)/shard_map/ppermute | solution.py:31
  73.4 9.1 %collective-permute-done.9.odd = bf16[4,88,768]{2,1,0:T(8,128)(2,1)S(1)} collective-permute-done((bf16[4,88,768]{2,1,0:T(8,128)(2,1)S(1)}, bf16[4,88,768]{2,1,0:T(8,128)(2,1)S(1)}, u32[]{:S(2)}, u32[]{:S(2)}) %collective-permute-start.9) | collective-permute-done | bytes 540704 | tf_op jit(solution)/shard_map/ppermute | solution.py:31
  88.4 2.7 %join.1.w_ref = bf16[1408,768]{1,0:T(8,128)(2,1)S(1)} custom-call(s32[4]{0:T(128)S(1)} %pad_add_fusion.scalars, bf16[4,88,768]{2,1,0:T(8,128)(2,1)S(1)} %pad_maximum_fusion.1.even, bf16[4,88,768]{2,1,0:T(8,128)(2,1)S(1)} %collective-permute-done.9.odd, bf16[4,88,768]{2,1,0:T(8,128)(2,1)S(1)} %collective-permute-done.10.even_far, ...), custom_call_target="tpu_custom_call" | custom-call | flops 1700000000 | bytes 5000000 | tf_op jit(solution)/shard_map/join/pallas_call | solution.py:337
  91.0 6.5 %collective-permute-done.25.refs_3_ = bf16[192,1408]{1,0:T(8,128)(2,1)S(1)} collective-permute-done((bf16[192,1408]{1,0:T(8,128)(2,1)S(1)}, bf16[192,1408]{1,0:T(8,128)(2,1)S(1)}, u32[]{:S(2)}, u32[]{:S(2)}) %collective-permute-start.25) | collective-permute-done | bytes 540704 | tf_op jit(solution)/shard_map/ppermute | solution.py:31
  100.3 2.7 %embed.3 = (bf16[1408,512]{1,0:T(8,128)(2,1)S(1)}, bf16[1408,512]{1,0:T(8,128)(2,1)}, f32[1,512]{1,0:T(1,128)}) custom-call(bf16[1408,768]{1,0:T(8,128)(2,1)S(1)} %join.1.w_ref, bf16[768,512]{1,0:T(8,128)(2,1)S(1)} %collective-permute-done.19.patch_ref), custom_call_target="tpu_custom_call" | custom-call | flops 1107296256 | bytes 6000000 | tf_op jit(solution)/shard_map/embed/pallas_call | solution.py:305
  104.5 6.7 %shard_map.95 = (bf16[768,512]{1,0:T(8,128)(2,1)S(1)}, bf16[768,512]{1,0:T(8,128)(2,1)S(1)}, bf16[768,1408]{1,0:T(8,128)(2,1)S(1)}, bf16[192,1408]{1,0:T(8,128)(...) custom-call(s32[4]{0:T(128)S(1)} %pad_add_fusion.scalars, ...), custom_call_target="tpu_custom_call" | custom-call | flops 4429185024 | bytes 15000000 | tf_op jit(solution)/shard_map/pallas_call | solution.py:448
  113.3 6.9 %shard_map.97 = (bf16[768,512]{1,0:T(8,128)(2,1)S(1)}, bf16[768,512]{1,0:T(8,128)(2,1)S(1)}, bf16[768,1408]{1,0:T(8,128)(2,1)S(1)}, bf16[96,1408]{1,0:T(8,128)(2...) custom-call(s32[4]{0:T(128)S(1)} %pad_add_fusion.scalars, ...), custom_call_target="tpu_custom_call" | custom-call | flops 4429185024 | bytes 15000000 | tf_op jit(solution)/shard_map/pallas_call | solution.py:448
  132.0 3.4 %tail.1 = (bf16[88,768]{1,0:T(8,128)(2,1)S(1)}, bf16[88,768]{1,0:T(8,128)(2,1)S(1)}, bf16[88,768]{1,0:T(8,128)(2,1)S(1)}, bf16[88,768]{1,0:T(8,128)(2,1)S(1)}, b...) custom-call(s32[4]{0:T(128)S(1)} %pad_add_fusion.scalars, ...), custom_call_target="tpu_custom_call" | custom-call | flops 1200000000 | bytes 9000000 | tf_op jit(solution)/shard_map/tail/pallas_call | solution.py:380
  135.3 5.5 %collective-permute-done.41 = bf16[96,1408]{1,0:T(8,128)(2,1)S(1)} collective-permute-done((bf16[96,1408]{1,0:T(8,128)(2,1)S(1)}, bf16[96,1408]{1,0:T(8,128)(2,1)S(1)}, u32[]{:S(2)}, u32[]{:S(2)}) %collective-permute-start.41) | collective-permute-done | bytes 270368 | tf_op jit(solution)/shard_map/ppermute | solution.py:31
  146.7 9.3 %collective-permute-done.42 = bf16[96,1408]{1,0:T(8,128)(2,1)S(1)} collective-permute-done((bf16[96,1408]{1,0:T(8,128)(2,1)S(1)}, bf16[96,1408]{1,0:T(8,128)(2,1)S(1)}, u32[]{:S(2)}, u32[]{:S(2)}) %collective-permute-start.42) | collective-permute-done | bytes 270368 | tf_op jit(solution)/shard_map/ppermute | solution.py:31
  159.7 3.2 %collective-permute-done.31 = bf16[88,768]{1,0:T(8,128)(2,1)S(1)} collective-permute-done((bf16[88,768]{1,0:T(8,128)(2,1)S(1)}, bf16[88,768]{1,0:T(8,128)(2,1)S(1)}, u32[]{:S(2)}, u32[]{:S(2)}) %collective-permute-start.31) | collective-permute-done | bytes 135200 | tf_op jit(solution)/shard_map/ppermute | solution.py:31
  162.9 2.6 %collective-permute-done.34 = bf16[88,768]{1,0:T(8,128)(2,1)S(1)} collective-permute-done((bf16[88,768]{1,0:T(8,128)(2,1)S(1)}, bf16[88,768]{1,0:T(8,128)(2,1)S(1)}, u32[]{:S(2)}, u32[]{:S(2)}) %collective-permute-start.34) | collective-permute-done | bytes 135200 | tf_op jit(solution)/shard_map/ppermute | solution.py:31
  167.0 3.0 %collective-permute-done.43 = bf16[96,1408]{1,0:T(8,128)(2,1)S(1)} collective-permute-done((bf16[96,1408]{1,0:T(8,128)(2,1)S(1)}, bf16[96,1408]{1,0:T(8,128)(2,1)S(1)}, u32[]{:S(2)}, u32[]{:S(2)}) %collective-permute-start.43) | collective-permute-done | bytes 270368 | tf_op jit(solution)/shard_map/ppermute | solution.py:31
  176.1 6.1 %collective-permute-done.36 = bf16[88,768]{1,0:T(8,128)(2,1)S(1)} collective-permute-done((bf16[88,768]{1,0:T(8,128)(2,1)S(1)}, bf16[88,768]{1,0:T(8,128)(2,1)S(1)}, u32[]{:S(2)}, u32[]{:S(2)}) %collective-permute-start.36) | collective-permute-done | bytes 135200 | tf_op jit(solution)/shard_map/ppermute | solution.py:31
  (144 shorter events, 68.3 us)
Async XLA Ops:
  0.7 36.5 %collective-permute-start.6 = (bf16[88,768]{1,0:T(8,128)(2,1)}, bf16[88,768]{1,0:T(8,128)(2,1)}, u32[]{:S(2)}, u32[]{:S(2)}) collective-permute-start(bf16[88,768]{1,0:T(8,128)(2,1)} %param.11), channel_id=1, source_target_pairs={{0,4},{2,6},{4,0},{6,2},{8,12},{10,14},{12,8},{14,10},{1,5},{3,7},... | collective-permute-start | bytes 405512 | tf_op jit(solution)/shard_map/ppermute | solution.py:31
  3.8 41.3 %collective-permute-start.7 = (bf16[88,768]{1,0:T(8,128)(2,1)}, bf16[88,768]{1,0:T(8,128)(2,1)}, u32[]{:S(2)}, u32[]{:S(2)}) collective-permute-start(bf16[88,768]{1,0:T(8,128)(2,1)} %param.11), channel_id=1, source_target_pairs={{0,8},{2,10},{4,12},{6,14},{8,0},{10,2},{12,4},{14,6},{1,9},{3,11}... | collective-permute-start | bytes 405512 | tf_op jit(solution)/shard_map/ppermute | solution.py:31
  14.9 30.2 %collective-permute-start.21 = (bf16[96,1408]{1,0:T(8,128)(2,1)}, bf16[96,1408]{1,0:T(8,128)(2,1)}, u32[]{:S(2)}, u32[]{:S(2)}) collective-permute-start(bf16[96,1408]{1,0:T(8,128)(2,1)} %constant_dynamic-slice_fusion), channel_id=1, source_target_pairs={{0,8},{2,10},{4,12},{6,14},{8,0},{10,2},{12,4},{14,6},{1,9},{3,11}... | collective-permute-start | bytes 811016 | tf_op jit(solution)/shard_map/ppermute | solution.py:31
  19.4 29.8 %collective-permute-start.8 = (bf16[88,768]{1,0:T(8,128)(2,1)}, bf16[88,768]{1,0:T(8,128)(2,1)}, u32[]{:S(2)}, u32[]{:S(2)}) collective-permute-start(bf16[88,768]{1,0:T(8,128)(2,1)} %param.11), channel_id=1, source_target_pairs={{0,12},{2,14},{4,8},{6,10},{8,4},{10,6},{12,0},{14,2},{1,13},{3,15... | collective-permute-start | bytes 405512 | tf_op jit(solution)/shard_map/ppermute | solution.py:31
  37.2 15.9 %collective-permute-start.13 = (bf16[384,128]{1,0:T(8,128)(2,1)}, bf16[384,128]{1,0:T(8,128)(2,1)}, u32[]{:S(2)}, u32[]{:S(2)}) collective-permute-start(bf16[384,128]{1,0:T(8,128)(2,1)} %get-tuple-element.52), channel_id=1, source_target_pairs={{0,4},{2,6},{4,0},{6,2},{8,12},{10,14},{12,8},{14,10},{1,5},{3,7},... | collective-permute-start | bytes 294920 | tf_op jit(solution)/shard_map/ppermute | solution.py:31
  45.1 20.0 %collective-permute-start.22 = (bf16[96,1408]{1,0:T(8,128)(2,1)}, bf16[96,1408]{1,0:T(8,128)(2,1)}, u32[]{:S(2)}, u32[]{:S(2)}) collective-permute-start(bf16[96,1408]{1,0:T(8,128)(2,1)} %collective-permute-done.21), channel_id=1, source_target_pairs={{0,16},{16,0},{1,17},{17,1},{2,18},{18,2},{3,19},{19,3},{4,20},{20... | collective-permute-start | bytes 811016 | tf_op jit(solution)/shard_map/ppermute | solution.py:31
  58.2 14.5 %collective-permute-start.2 = (bf16[192,1408]{1,0:T(8,128)(2,1)S(1)}, bf16[192,1408]{1,0:T(8,128)(2,1)S(1)}, u32[]{:S(2)}, u32[]{:S(2)}) collective-permute-start(bf16[192,1408]{1,0:T(8,128)(2,1)S(1)} %copy-done.4), channel_id=1, source_target_pairs={{0,2},{2,0},{4,6},{6,4},{8,10},{10,8},{12,14},{14,12},{1,3},{3,1},... | collective-permute-start | bytes 1622024 | tf_op jit(solution)/shard_map/ppermute | solution.py:31
  60.2 44.3 %collective-permute-start.20 = (bf16[4,192,512]{2,1,0:T(8,128)(2,1)S(1)}, bf16[4,192,512]{2,1,0:T(8,128)(2,1)S(1)}, u32[]{:S(2)}, u32[]{:S(2)}) collective-permute-start(bf16[4,192,512]{2,1,0:T(8,128)(2,1)S(1)} %get-tuple-element.62), channel_id=1, source_target_pairs={{0,1},{1,0},{2,3},{3,2},{4,5},{5,4},{6,7},{7,6},{8,9},{9,8},{10,11... | collective-permute-start | bytes 2359304 | tf_op jit(solution)/shard_map/ppermute | solution.py:31
  62.2 20.2 %collective-permute-start.9 = (bf16[4,88,768]{2,1,0:T(8,128)(2,1)S(1)}, bf16[4,88,768]{2,1,0:T(8,128)(2,1)S(1)}, u32[]{:S(2)}, u32[]{:S(2)}) collective-permute-start(bf16[4,88,768]{2,1,0:T(8,128)(2,1)S(1)} %pad_maximum_fusion.1.even), channel_id=1, source_target_pairs={{0,2},{2,0},{4,6},{6,4},{8,10},{10,8},{12,14},{14,12},{1,3},{3,1},... | collective-permute-start | bytes 1622024 | tf_op jit(solution)/shard_map/ppermute | solution.py:31
  65.1 17.4 %collective-permute-start.10 = (bf16[4,88,768]{2,1,0:T(8,128)(2,1)S(1)}, bf16[4,88,768]{2,1,0:T(8,128)(2,1)S(1)}, u32[]{:S(2)}, u32[]{:S(2)}) collective-permute-start(bf16[4,88,768]{2,1,0:T(8,128)(2,1)S(1)} %pad_maximum_fusion.1.even), channel_id=1, source_target_pairs={{0,1},{1,0},{2,3},{3,2},{4,5},{5,4},{6,7},{7,6},{8,9},{9,8},{10,11... | collective-permute-start | bytes 1622024 | tf_op jit(solution)/shard_map/ppermute | solution.py:31
  68.2 18.6 %collective-permute-start.19 = (bf16[768,512]{1,0:T(8,128)(2,1)S(1)}, bf16[768,512]{1,0:T(8,128)(2,1)S(1)}, u32[]{:S(2)}, u32[]{:S(2)}) collective-permute-start(bf16[768,512]{1,0:T(8,128)(2,1)S(1)} %get-tuple-element.58.patch_ref), channel_id=1, source_target_pairs={{0,1},{1,0},{2,3},{3,2},{4,5},{5,4},{6,7},{7,6},{8,9},{9,8},{10,11... | collective-permute-start | bytes 2359304 | tf_op jit(solution)/shard_map/ppermute | solution.py:31
  82.5 15.0 %collective-permute-start.25 = (bf16[192,1408]{1,0:T(8,128)(2,1)S(1)}, bf16[192,1408]{1,0:T(8,128)(2,1)S(1)}, u32[]{:S(2)}, u32[]{:S(2)}) collective-permute-start(bf16[192,1408]{1,0:T(8,128)(2,1)S(1)} %pad_maximum_fusion.refs_0_), channel_id=1, source_target_pairs={{0,4},{2,6},{4,0},{6,2},{8,12},{10,14},{12,8},{14,10},{1,5},{3,7},... | collective-permute-start | bytes 1622024 | tf_op jit(solution)/shard_map/ppermute | solution.py:31
  86.3 27.0 %collective-permute-start.27 = (bf16[4,192,512]{2,1,0:T(8,128)(2,1)S(1)}, bf16[4,192,512]{2,1,0:T(8,128)(2,1)S(1)}, u32[]{:S(2)}, u32[]{:S(2)}) collective-permute-start(bf16[4,192,512]{2,1,0:T(8,128)(2,1)S(1)} %get-tuple-element.66), channel_id=1, source_target_pairs={{0,1},{1,0},{2,3},{3,2},{4,5},{5,4},{6,7},{7,6},{8,9},{9,8},{10,11... | collective-permute-start | bytes 2359304 | tf_op jit(solution)/shard_map/ppermute | solution.py:31
  86.7 16.3 %collective-permute-start.23 = (bf16[96,1408]{1,0:T(8,128)(2,1)S(1)}, bf16[96,1408]{1,0:T(8,128)(2,1)S(1)}, u32[]{:S(2)}, u32[]{:S(2)}) collective-permute-start(bf16[96,1408]{1,0:T(8,128)(2,1)S(1)} %fusion.3), channel_id=1, source_target_pairs={{0,2},{2,0},{4,6},{6,4},{8,10},{10,8},{12,14},{14,12},{1,3},{3,1},... | collective-permute-start | bytes 811016 | tf_op jit(solution)/shard_map/ppermute | solution.py:31
  87.8 16.7 %collective-permute-start.5 = (bf16[96,1408]{1,0:T(8,128)(2,1)S(1)}, bf16[96,1408]{1,0:T(8,128)(2,1)S(1)}, u32[]{:S(2)}, u32[]{:S(2)}) collective-permute-start(bf16[96,1408]{1,0:T(8,128)(2,1)S(1)} %collective-permute-done.4.refs_3_), channel_id=1, source_target_pairs={{0,16},{16,0},{1,17},{17,1},{2,18},{18,2},{3,19},{19,3},{4,20},{20... | collective-permute-start | bytes 811016 | tf_op jit(solution)/shard_map/ppermute | solution.py:31
  97.5 15.8 %collective-permute-start.26 = (bf16[192,1408]{1,0:T(8,128)(2,1)S(1)}, bf16[192,1408]{1,0:T(8,128)(2,1)S(1)}, u32[]{:S(2)}, u32[]{:S(2)}) collective-permute-start(bf16[192,1408]{1,0:T(8,128)(2,1)S(1)} %collective-permute-done.25.refs_3_), channel_id=1, source_target_pairs={{0,2},{2,0},{4,6},{6,4},{8,10},{10,8},{12,14},{14,12},{1,3},{3,1},... | collective-permute-start | bytes 1622024 | tf_op jit(solution)/shard_map/ppermute | solution.py:31
  111.2 16.6 %collective-permute-start.38 = (bf16[192,1408]{1,0:T(8,128)(2,1)S(1)}, bf16[192,1408]{1,0:T(8,128)(2,1)S(1)}, u32[]{:S(2)}, u32[]{:S(2)}) collective-permute-start(bf16[192,1408]{1,0:T(8,128)(2,1)S(1)} %get-tuple-element.86), channel_id=1, source_target_pairs={{0,4},{2,6},{4,0},{6,2},{8,12},{10,14},{12,8},{14,10},{1,5},{3,7},... | collective-permute-start | bytes 1622024 | tf_op jit(solution)/shard_map/ppermute | solution.py:31
  112.1 45.2 %collective-permute-start.37 = (bf16[192,1408]{1,0:T(8,128)(2,1)S(1)}, bf16[192,1408]{1,0:T(8,128)(2,1)S(1)}, u32[]{:S(2)}, u32[]{:S(2)}) collective-permute-start(bf16[192,1408]{1,0:T(8,128)(2,1)S(1)} %get-tuple-element.84), channel_id=1, source_target_pairs={{0,4},{2,6},{4,0},{6,2},{8,12},{10,14},{12,8},{14,10},{1,5},{3,7},... | collective-permute-start | bytes 1622024 | tf_op jit(solution)/shard_map/ppermute | solution.py:31
  120.7 20.3 %collective-permute-start.44 = (bf16[96,1408]{1,0:T(8,128)(2,1)S(1)}, bf16[96,1408]{1,0:T(8,128)(2,1)S(1)}, u32[]{:S(2)}, u32[]{:S(2)}) collective-permute-start(bf16[96,1408]{1,0:T(8,128)(2,1)S(1)} %get-tuple-element.92), channel_id=1, source_target_pairs={{0,2},{2,0},{4,6},{6,4},{8,10},{10,8},{12,14},{14,12},{1,3},{3,1},... | collective-permute-start | bytes 811016 | tf_op jit(solution)/shard_map/ppermute | solution.py:31
  129.7 15.5 %collective-permute-start.40 = (bf16[96,1408]{1,0:T(8,128)(2,1)S(1)}, bf16[96,1408]{1,0:T(8,128)(2,1)S(1)}, u32[]{:S(2)}, u32[]{:S(2)}) collective-permute-start(bf16[96,1408]{1,0:T(8,128)(2,1)S(1)} %get-tuple-element.88), channel_id=1, source_target_pairs={{0,2},{2,0},{4,6},{6,4},{8,10},{10,8},{12,14},{14,12},{1,3},{3,1},... | collective-permute-start | bytes 811016 | tf_op jit(solution)/shard_map/ppermute | solution.py:31
  140.9 15.4 %collective-permute-start.29 = (bf16[704,768]{1,0:T(8,128)(2,1)S(1)}, bf16[704,768]{1,0:T(8,128)(2,1)S(1)}, u32[]{:S(2)}, u32[]{:S(2)}) collective-permute-start(bf16[704,768]{1,0:T(8,128)(2,1)S(1)} %get-tuple-element.75), channel_id=1, source_target_pairs={{0,1},{1,0},{2,3},{3,2},{4,5},{5,4},{6,7},{7,6},{8,9},{9,8},{10,11... | collective-permute-start | bytes 3244040 | tf_op jit(solution)/shard_map/ppermute | solution.py:31
  141.0 17.5 %collective-permute-start.39 = (bf16[192,1408]{1,0:T(8,128)(2,1)S(1)}, bf16[192,1408]{1,0:T(8,128)(2,1)S(1)}, u32[]{:S(2)}, u32[]{:S(2)}) collective-permute-start(bf16[192,1408]{1,0:T(8,128)(2,1)S(1)} %add_convert_fusion.1), channel_id=1, source_target_pairs={{0,2},{2,0},{4,6},{6,4},{8,10},{10,8},{12,14},{14,12},{1,3},{3,1},... | collective-permute-start | bytes 1622024 | tf_op jit(solution)/shard_map/ppermute | solution.py:31
  142.0 14.1 %collective-permute-start.42 = (bf16[96,1408]{1,0:T(8,128)(2,1)S(1)}, bf16[96,1408]{1,0:T(8,128)(2,1)S(1)}, u32[]{:S(2)}, u32[]{:S(2)}) collective-permute-start(bf16[96,1408]{1,0:T(8,128)(2,1)S(1)} %add_convert_fusion.7), channel_id=1, source_target_pairs={{0,4},{2,6},{4,0},{6,2},{8,12},{10,14},{12,8},{14,10},{1,5},{3,7},... | collective-permute-start | bytes 811016 | tf_op jit(solution)/shard_map/ppermute | solution.py:31
  145.1 21.9 %collective-permute-start.47 = (bf16[96,1408]{1,0:T(8,128)(2,1)S(1)}, bf16[96,1408]{1,0:T(8,128)(2,1)S(1)}, u32[]{:S(2)}, u32[]{:S(2)}) collective-permute-start(bf16[96,1408]{1,0:T(8,128)(2,1)S(1)} %add_convert_fusion.3), channel_id=1, source_target_pairs={{0,8},{2,10},{4,12},{6,14},{8,0},{10,2},{12,4},{14,6},{1,9},{3,11}... | collective-permute-start | bytes 811016 | tf_op jit(solution)/shard_map/ppermute | solution.py:31
  (40 other events, 372.0 us)

commit v3 on v2

--- a/solution.py
+++ b/solution.py
@@ -88,7 +88,7 @@
             self_x[kind, row] = value
         return carry
 
-    lax.fori_loop(0, total - 1, x_faces, 0)
+    lax.fori_loop(0, total - 1, x_faces, 0, unroll=3)
 
     strain = [[loading[case, c, a] for a in range(3)] for c in range(3)]
 
@@ -123,7 +123,7 @@
             even[c, row] = forcing * inverse
         return carry
 
-    lax.fori_loop(1, total - 1, setup, 0, unroll=2)
+    lax.fori_loop(1, total - 1, setup, 0, unroll=7)
 
     buffers = (even, odd)
     for step in range(1, SWEEPS):
@@ -150,7 +150,7 @@
                     displace_ref[c, row - halo] = value
             return carry
 
-        lax.fori_loop(1 + step, total - 1 - step, sweep, 0, unroll=2)
+        lax.fori_loop(1 + step, total - 1 - step, sweep, 0, unroll=4)
 
     band_rows = ny // bands
     for k in range(bands):
@@ -315,7 +315,6 @@
         cost_estimate=pl.CostEstimate(
             flops=2 * model * features * tokens, bytes_accessed=6_000_000, transcendentals=0
         ),
-        name="embed",
     )(w_all, patches)
 
 

time: 183 us -> 183 us (level)
  no operation moved by 1% of the time
where the time goes in v3:
time: 183 us
  waiting for transfers between devices  60.7 us (33%)
  starting transfers between devices  59.5 us (33%)
  Pallas kernels  40.2 us (22%)
  other arithmetic  8.84 us (5%)
  local copies, waits for them, and re-layouts  6.19 us (3%)
  matrix products  5.42 us (3%)
    ppermute x46, waiting for transfers between devices, exchange(): return lax.ppermute(value, axis, [(i, i ^ bit) for i in range(size)])  60.7 us
    ppermute x46, starting transfers between devices, exchange(): return lax.ppermute(value, axis, [(i, i ^ bit) for i in range(size)])  54.5 us
    pallas_call x2, Pallas kernels, mlp(): pl.pallas_call(partial(mlp_kernel, picks=picks, count=count), grid=(1,),...  13.6 us
    pallas_call x1, Pallas kernels, solve(): pl.pallas_call(partial(solver_kernel, slab=slab, bands=bands, patch_y=PAT...  10.5 us
    dot_general x4, matrix products, contract(): lax.dot_general(left, right, (((left_dim,), (right_dim,)), ((), ())), pre...  5.42 us
    pallas_call x2, Pallas kernels, embed(): pl.pallas_call(embed_kernel, out_shape=[jax.ShapeDtypeStruct((model, toke...  4.47 us
    unnamed x33, local copies, waits for them, and re-layouts  3.76 us
    ppermute x1, starting transfers between devices, local(): before = lax.ppermute(small[slab - SWEEPS:], 'dev', up)  3.68 us
  transfers between devices with their start and end apart: 48, of which 18 were waited for; matrix products, arithmetic and copies ran while one was open for 9% of the time, Pallas kernels for 22%

profile of v3, /device:TPU:0, one launch (start us, length us, event | category | flops | bytes accessed | tf_op | source)
XLA Modules:
  0.0 182.5 jit_solution(5246575864189859105)
XLA Ops:
  0.7 3.1 %collective-permute-start.6 = (bf16[88,768]{1,0:T(8,128)(2,1)}, bf16[88,768]{1,0:T(8,128)(2,1)}, u32[]{:S(2)}, u32[]{:S(2)}) collective-permute-start(bf16[88,768]{1,0:T(8,128)(2,1)} %param.11), channel_id=1, source_target_pairs={{0,4},{2,6},{4,0},{6,2},{8,12},{10,14},{12,8},{14,10},{1,5},{3,7},... | collective-permute-start | bytes 405512 | tf_op jit(solution)/shard_map/ppermute | solution.py:31
  3.8 2.6 %collective-permute-start.7 = (bf16[88,768]{1,0:T(8,128)(2,1)}, bf16[88,768]{1,0:T(8,128)(2,1)}, u32[]{:S(2)}, u32[]{:S(2)}) collective-permute-start(bf16[88,768]{1,0:T(8,128)(2,1)} %param.11), channel_id=1, source_target_pairs={{0,8},{2,10},{4,12},{6,14},{8,0},{10,2},{12,4},{14,6},{1,9},{3,11}... | collective-permute-start | bytes 405512 | tf_op jit(solution)/shard_map/ppermute | solution.py:31
  8.2 3.7 %collective-permute-start = (bf16[4,128,128]{2,1,0:T(8,128)(2,1)}, bf16[4,128,128]{2,1,0:T(8,128)(2,1)S(1)}, u32[]{:S(2)}, u32[]{:S(2)}) collective-permute-start(bf16[4,128,128]{2,1,0:T(8,128)(2,1)} %get-tuple-element.106), channel_id=1, source_target_pairs={{0,2},{2,4},{4,6},{6,8},{8,10},{10,12},{12,14},{1,3},{3,5},{5,7},{... | collective-permute-start | bytes 393224 | tf_op jit(solution)/shard_map/ppermute | solution.py:522
  14.9 2.4 %collective-permute-start.21 = (bf16[96,1408]{1,0:T(8,128)(2,1)}, bf16[96,1408]{1,0:T(8,128)(2,1)}, u32[]{:S(2)}, u32[]{:S(2)}) collective-permute-start(bf16[96,1408]{1,0:T(8,128)(2,1)} %constant_dynamic-slice_fusion), channel_id=1, source_target_pairs={{0,8},{2,10},{4,12},{6,14},{8,0},{10,2},{12,4},{14,6},{1,9},{3,11}... | collective-permute-start | bytes 811016 | tf_op jit(solution)/shard_map/ppermute | solution.py:31
  19.4 2.5 %collective-permute-start.8 = (bf16[88,768]{1,0:T(8,128)(2,1)}, bf16[88,768]{1,0:T(8,128)(2,1)}, u32[]{:S(2)}, u32[]{:S(2)}) collective-permute-start(bf16[88,768]{1,0:T(8,128)(2,1)} %param.11), channel_id=1, source_target_pairs={{0,12},{2,14},{4,8},{6,10},{8,4},{10,6},{12,0},{14,2},{1,13},{3,15... | collective-permute-start | bytes 405512 | tf_op jit(solution)/shard_map/ppermute | solution.py:31
  23.0 10.5 %solver.1 = (f32[3,8,128,128]{3,2,1,0:T(8,128)}, bf16[384,128]{1,0:T(8,128)(2,1)S(1)}, bf16[384,128]{1,0:T(8,128)(2,1)}, bf16[384,128]{1,0:T(8,128)(2,1)}, bf16[...) custom-call(s32[4]{0:T(128)S(1)} %pad_add_fusion.scalars, ...), custom_call_target="tpu_custom_call" | custom-call | flops 40000000 | bytes 4000000 | tf_op jit(solution)/shard_map/solver/pallas_call | solution.py:177
  36.6 7.9 %collective-permute-start.13 = (bf16[384,128]{1,0:T(8,128)(2,1)}, bf16[384,128]{1,0:T(8,128)(2,1)}, u32[]{:S(2)}, u32[]{:S(2)}) collective-permute-start(bf16[384,128]{1,0:T(8,128)(2,1)} %get-tuple-element.52), channel_id=1, source_target_pairs={{0,4},{2,6},{4,0},{6,2},{8,12},{10,14},{12,8},{14,10},{1,5},{3,7},... | collective-permute-start | bytes 294920 | tf_op jit(solution)/shard_map/ppermute | solution.py:31
  49.6 2.9 %collective-permute-start.16 = (bf16[384,128]{1,0:T(8,128)(2,1)S(1)}, bf16[384,128]{1,0:T(8,128)(2,1)S(1)}, u32[]{:S(2)}, u32[]{:S(2)}) collective-permute-start(bf16[384,128]{1,0:T(8,128)(2,1)S(1)} %copy-done.11), channel_id=1, source_target_pairs={{0,10},{2,8},{4,14},{6,12},{8,2},{10,0},{12,6},{14,4},{1,11},{3,9}... | collective-permute-start | bytes 294920 | tf_op jit(solution)/shard_map/ppermute | solution.py:31
  54.0 2.3 %collective-permute-start.18 = (bf16[384,128]{1,0:T(8,128)(2,1)S(1)}, bf16[384,128]{1,0:T(8,128)(2,1)S(1)}, u32[]{:S(2)}, u32[]{:S(2)}) collective-permute-start(bf16[384,128]{1,0:T(8,128)(2,1)S(1)} %copy-done.7), channel_id=1, source_target_pairs={{0,14},{2,12},{4,10},{6,8},{8,6},{10,4},{12,2},{14,0},{1,15},{3,13... | collective-permute-start | bytes 294920 | tf_op jit(solution)/shard_map/ppermute | solution.py:31
  62.2 2.3 %patchify.1 = (bf16[768,512]{1,0:T(8,128)(2,1)S(1)}, bf16[768,512]{1,0:T(8,128)(2,1)S(1)}) custom-call(s32[4]{0:T(128)S(1)} %pad_add_fusion.scalars, bf16[384,128]{1,0:T(8,128)(2,1)S(1)} %get-tuple-element.50.refs_0_, bf16[384,128]{1,0:T(8,128)(2,1)S(1)} %collective-permute-done.12.refs_1_, bf16[384,128]{1,0:T(8,128)(2,1)} %collective-permute-done.13.refs_2_, ...), custom_call_target="tpu_custom_call" | custom-call | flops 1000000000 | bytes 5000000 | tf_op jit(solution)/shard_map/patchify/pallas_call | solution.py:238
  67.6 4.5 %collective-permute-done.2.refs_1_ = bf16[192,1408]{1,0:T(8,128)(2,1)S(1)} collective-permute-done((bf16[192,1408]{1,0:T(8,128)(2,1)S(1)}, bf16[192,1408]{1,0:T(8,128)(2,1)S(1)}, u32[]{:S(2)}, u32[]{:S(2)}) %collective-permute-start.2) | collective-permute-done | bytes 540704 | tf_op jit(solution)/shard_map/ppermute | solution.py:31
  72.9 9.1 %collective-permute-done.9.odd = bf16[4,88,768]{2,1,0:T(8,128)(2,1)S(1)} collective-permute-done((bf16[4,88,768]{2,1,0:T(8,128)(2,1)S(1)}, bf16[4,88,768]{2,1,0:T(8,128)(2,1)S(1)}, u32[]{:S(2)}, u32[]{:S(2)}) %collective-permute-start.9) | collective-permute-done | bytes 540704 | tf_op jit(solution)/shard_map/ppermute | solution.py:31
  87.8 2.7 %join.1.w_ref = bf16[1408,768]{1,0:T(8,128)(2,1)S(1)} custom-call(s32[4]{0:T(128)S(1)} %pad_add_fusion.scalars, bf16[4,88,768]{2,1,0:T(8,128)(2,1)S(1)} %pad_maximum_fusion.1.even, bf16[4,88,768]{2,1,0:T(8,128)(2,1)S(1)} %collective-permute-done.9.odd, bf16[4,88,768]{2,1,0:T(8,128)(2,1)S(1)} %collective-permute-done.10.even_far, ...), custom_call_target="tpu_custom_call" | custom-call | flops 1700000000 | bytes 5000000 | tf_op jit(solution)/shard_map/join/pallas_call | solution.py:336
  90.5 6.5 %collective-permute-done.25.refs_3_ = bf16[192,1408]{1,0:T(8,128)(2,1)S(1)} collective-permute-done((bf16[192,1408]{1,0:T(8,128)(2,1)S(1)}, bf16[192,1408]{1,0:T(8,128)(2,1)S(1)}, u32[]{:S(2)}, u32[]{:S(2)}) %collective-permute-start.25) | collective-permute-done | bytes 540704 | tf_op jit(solution)/shard_map/ppermute | solution.py:31
  99.7 2.7 %shard_map.95 = (bf16[1408,512]{1,0:T(8,128)(2,1)S(1)}, bf16[1408,512]{1,0:T(8,128)(2,1)}, f32[1,512]{1,0:T(1,128)}) custom-call(bf16[1408,768]{1,0:T(8,128)(2,1)S(1)} %join.1.w_ref, bf16[768,512]{1,0:T(8,128)(2,1)S(1)} %collective-permute-done.19.patch_ref), custom_call_target="tpu_custom_call" | custom-call | flops 1107296256 | bytes 6000000 | tf_op jit(solution)/shard_map/pallas_call | solution.py:305
  103.9 6.7 %shard_map.97 = (bf16[768,512]{1,0:T(8,128)(2,1)S(1)}, bf16[768,512]{1,0:T(8,128)(2,1)S(1)}, bf16[768,1408]{1,0:T(8,128)(2,1)S(1)}, bf16[192,1408]{1,0:T(8,128)(...) custom-call(s32[4]{0:T(128)S(1)} %pad_add_fusion.scalars, ...), custom_call_target="tpu_custom_call" | custom-call | flops 4429185024 | bytes 15000000 | tf_op jit(solution)/shard_map/pallas_call | solution.py:447
  112.8 6.9 %shard_map.99 = (bf16[768,512]{1,0:T(8,128)(2,1)S(1)}, bf16[768,512]{1,0:T(8,128)(2,1)S(1)}, bf16[768,1408]{1,0:T(8,128)(2,1)S(1)}, bf16[96,1408]{1,0:T(8,128)(2...) custom-call(s32[4]{0:T(128)S(1)} %pad_add_fusion.scalars, ...), custom_call_target="tpu_custom_call" | custom-call | flops 4429185024 | bytes 15000000 | tf_op jit(solution)/shard_map/pallas_call | solution.py:447
  131.4 3.4 %tail.1 = (bf16[88,768]{1,0:T(8,128)(2,1)S(1)}, bf16[88,768]{1,0:T(8,128)(2,1)S(1)}, bf16[88,768]{1,0:T(8,128)(2,1)S(1)}, bf16[88,768]{1,0:T(8,128)(2,1)S(1)}, b...) custom-call(s32[4]{0:T(128)S(1)} %pad_add_fusion.scalars, ...), custom_call_target="tpu_custom_call" | custom-call | flops 1200000000 | bytes 9000000 | tf_op jit(solution)/shard_map/tail/pallas_call | solution.py:379
  134.7 5.5 %collective-permute-done.41 = bf16[96,1408]{1,0:T(8,128)(2,1)S(1)} collective-permute-done((bf16[96,1408]{1,0:T(8,128)(2,1)S(1)}, bf16[96,1408]{1,0:T(8,128)(2,1)S(1)}, u32[]{:S(2)}, u32[]{:S(2)}) %collective-permute-start.41) | collective-permute-done | bytes 270368 | tf_op jit(solution)/shard_map/ppermute | solution.py:31
  146.1 9.4 %collective-permute-done.42 = bf16[96,1408]{1,0:T(8,128)(2,1)S(1)} collective-permute-done((bf16[96,1408]{1,0:T(8,128)(2,1)S(1)}, bf16[96,1408]{1,0:T(8,128)(2,1)S(1)}, u32[]{:S(2)}, u32[]{:S(2)}) %collective-permute-start.42) | collective-permute-done | bytes 270368 | tf_op jit(solution)/shard_map/ppermute | solution.py:31
  159.1 3.3 %collective-permute-done.31 = bf16[88,768]{1,0:T(8,128)(2,1)S(1)} collective-permute-done((bf16[88,768]{1,0:T(8,128)(2,1)S(1)}, bf16[88,768]{1,0:T(8,128)(2,1)S(1)}, u32[]{:S(2)}, u32[]{:S(2)}) %collective-permute-start.31) | collective-permute-done | bytes 135200 | tf_op jit(solution)/shard_map/ppermute | solution.py:31
  162.4 2.6 %collective-permute-done.34 = bf16[88,768]{1,0:T(8,128)(2,1)S(1)} collective-permute-done((bf16[88,768]{1,0:T(8,128)(2,1)S(1)}, bf16[88,768]{1,0:T(8,128)(2,1)S(1)}, u32[]{:S(2)}, u32[]{:S(2)}) %collective-permute-start.34) | collective-permute-done | bytes 135200 | tf_op jit(solution)/shard_map/ppermute | solution.py:31
  166.4 3.1 %collective-permute-done.43 = bf16[96,1408]{1,0:T(8,128)(2,1)S(1)} collective-permute-done((bf16[96,1408]{1,0:T(8,128)(2,1)S(1)}, bf16[96,1408]{1,0:T(8,128)(2,1)S(1)}, u32[]{:S(2)}, u32[]{:S(2)}) %collective-permute-start.43) | collective-permute-done | bytes 270368 | tf_op jit(solution)/shard_map/ppermute | solution.py:31
  175.5 6.2 %collective-permute-done.36 = bf16[88,768]{1,0:T(8,128)(2,1)S(1)} collective-permute-done((bf16[88,768]{1,0:T(8,128)(2,1)S(1)}, bf16[88,768]{1,0:T(8,128)(2,1)S(1)}, u32[]{:S(2)}, u32[]{:S(2)}) %collective-permute-start.36) | collective-permute-done | bytes 135200 | tf_op jit(solution)/shard_map/ppermute | solution.py:31
  (144 shorter events, 68.2 us)
Async XLA Ops:
  0.7 36.0 %collective-permute-start.6 = (bf16[88,768]{1,0:T(8,128)(2,1)}, bf16[88,768]{1,0:T(8,128)(2,1)}, u32[]{:S(2)}, u32[]{:S(2)}) collective-permute-start(bf16[88,768]{1,0:T(8,128)(2,1)} %param.11), channel_id=1, source_target_pairs={{0,4},{2,6},{4,0},{6,2},{8,12},{10,14},{12,8},{14,10},{1,5},{3,7},... | collective-permute-start | bytes 405512 | tf_op jit(solution)/shard_map/ppermute | solution.py:31
  3.8 40.8 %collective-permute-start.7 = (bf16[88,768]{1,0:T(8,128)(2,1)}, bf16[88,768]{1,0:T(8,128)(2,1)}, u32[]{:S(2)}, u32[]{:S(2)}) collective-permute-start(bf16[88,768]{1,0:T(8,128)(2,1)} %param.11), channel_id=1, source_target_pairs={{0,8},{2,10},{4,12},{6,14},{8,0},{10,2},{12,4},{14,6},{1,9},{3,11}... | collective-permute-start | bytes 405512 | tf_op jit(solution)/shard_map/ppermute | solution.py:31
  14.9 29.7 %collective-permute-start.21 = (bf16[96,1408]{1,0:T(8,128)(2,1)}, bf16[96,1408]{1,0:T(8,128)(2,1)}, u32[]{:S(2)}, u32[]{:S(2)}) collective-permute-start(bf16[96,1408]{1,0:T(8,128)(2,1)} %constant_dynamic-slice_fusion), channel_id=1, source_target_pairs={{0,8},{2,10},{4,12},{6,14},{8,0},{10,2},{12,4},{14,6},{1,9},{3,11}... | collective-permute-start | bytes 811016 | tf_op jit(solution)/shard_map/ppermute | solution.py:31
  19.4 29.3 %collective-permute-start.8 = (bf16[88,768]{1,0:T(8,128)(2,1)}, bf16[88,768]{1,0:T(8,128)(2,1)}, u32[]{:S(2)}, u32[]{:S(2)}) collective-permute-start(bf16[88,768]{1,0:T(8,128)(2,1)} %param.11), channel_id=1, source_target_pairs={{0,12},{2,14},{4,8},{6,10},{8,4},{10,6},{12,0},{14,2},{1,13},{3,15... | collective-permute-start | bytes 405512 | tf_op jit(solution)/shard_map/ppermute | solution.py:31
  36.6 15.9 %collective-permute-start.13 = (bf16[384,128]{1,0:T(8,128)(2,1)}, bf16[384,128]{1,0:T(8,128)(2,1)}, u32[]{:S(2)}, u32[]{:S(2)}) collective-permute-start(bf16[384,128]{1,0:T(8,128)(2,1)} %get-tuple-element.52), channel_id=1, source_target_pairs={{0,4},{2,6},{4,0},{6,2},{8,12},{10,14},{12,8},{14,10},{1,5},{3,7},... | collective-permute-start | bytes 294920 | tf_op jit(solution)/shard_map/ppermute | solution.py:31
  44.5 20.0 %collective-permute-start.22 = (bf16[96,1408]{1,0:T(8,128)(2,1)}, bf16[96,1408]{1,0:T(8,128)(2,1)}, u32[]{:S(2)}, u32[]{:S(2)}) collective-permute-start(bf16[96,1408]{1,0:T(8,128)(2,1)} %collective-permute-done.21), channel_id=1, source_target_pairs={{0,16},{16,0},{1,17},{17,1},{2,18},{18,2},{3,19},{19,3},{4,20},{20... | collective-permute-start | bytes 811016 | tf_op jit(solution)/shard_map/ppermute | solution.py:31
  57.6 14.5 %collective-permute-start.2 = (bf16[192,1408]{1,0:T(8,128)(2,1)S(1)}, bf16[192,1408]{1,0:T(8,128)(2,1)S(1)}, u32[]{:S(2)}, u32[]{:S(2)}) collective-permute-start(bf16[192,1408]{1,0:T(8,128)(2,1)S(1)} %copy-done.4), channel_id=1, source_target_pairs={{0,2},{2,0},{4,6},{6,4},{8,10},{10,8},{12,14},{14,12},{1,3},{3,1},... | collective-permute-start | bytes 1622024 | tf_op jit(solution)/shard_map/ppermute | solution.py:31
  59.7 44.3 %collective-permute-start.20 = (bf16[4,192,512]{2,1,0:T(8,128)(2,1)S(1)}, bf16[4,192,512]{2,1,0:T(8,128)(2,1)S(1)}, u32[]{:S(2)}, u32[]{:S(2)}) collective-permute-start(bf16[4,192,512]{2,1,0:T(8,128)(2,1)S(1)} %get-tuple-element.62), channel_id=1, source_target_pairs={{0,1},{1,0},{2,3},{3,2},{4,5},{5,4},{6,7},{7,6},{8,9},{9,8},{10,11... | collective-permute-start | bytes 2359304 | tf_op jit(solution)/shard_map/ppermute | solution.py:31
  61.7 20.2 %collective-permute-start.9 = (bf16[4,88,768]{2,1,0:T(8,128)(2,1)S(1)}, bf16[4,88,768]{2,1,0:T(8,128)(2,1)S(1)}, u32[]{:S(2)}, u32[]{:S(2)}) collective-permute-start(bf16[4,88,768]{2,1,0:T(8,128)(2,1)S(1)} %pad_maximum_fusion.1.even), channel_id=1, source_target_pairs={{0,2},{2,0},{4,6},{6,4},{8,10},{10,8},{12,14},{14,12},{1,3},{3,1},... | collective-permute-start | bytes 1622024 | tf_op jit(solution)/shard_map/ppermute | solution.py:31
  64.5 17.4 %collective-permute-start.10 = (bf16[4,88,768]{2,1,0:T(8,128)(2,1)S(1)}, bf16[4,88,768]{2,1,0:T(8,128)(2,1)S(1)}, u32[]{:S(2)}, u32[]{:S(2)}) collective-permute-start(bf16[4,88,768]{2,1,0:T(8,128)(2,1)S(1)} %pad_maximum_fusion.1.even), channel_id=1, source_target_pairs={{0,1},{1,0},{2,3},{3,2},{4,5},{5,4},{6,7},{7,6},{8,9},{9,8},{10,11... | collective-permute-start | bytes 1622024 | tf_op jit(solution)/shard_map/ppermute | solution.py:31
  67.6 18.6 %collective-permute-start.19 = (bf16[768,512]{1,0:T(8,128)(2,1)S(1)}, bf16[768,512]{1,0:T(8,128)(2,1)S(1)}, u32[]{:S(2)}, u32[]{:S(2)}) collective-permute-start(bf16[768,512]{1,0:T(8,128)(2,1)S(1)} %get-tuple-element.58.patch_ref), channel_id=1, source_target_pairs={{0,1},{1,0},{2,3},{3,2},{4,5},{5,4},{6,7},{7,6},{8,9},{9,8},{10,11... | collective-permute-start | bytes 2359304 | tf_op jit(solution)/shard_map/ppermute | solution.py:31
  82.0 15.0 %collective-permute-start.25 = (bf16[192,1408]{1,0:T(8,128)(2,1)S(1)}, bf16[192,1408]{1,0:T(8,128)(2,1)S(1)}, u32[]{:S(2)}, u32[]{:S(2)}) collective-permute-start(bf16[192,1408]{1,0:T(8,128)(2,1)S(1)} %pad_maximum_fusion.refs_0_), channel_id=1, source_target_pairs={{0,4},{2,6},{4,0},{6,2},{8,12},{10,14},{12,8},{14,10},{1,5},{3,7},... | collective-permute-start | bytes 1622024 | tf_op jit(solution)/shard_map/ppermute | solution.py:31
  85.7 27.1 %collective-permute-start.27 = (bf16[4,192,512]{2,1,0:T(8,128)(2,1)S(1)}, bf16[4,192,512]{2,1,0:T(8,128)(2,1)S(1)}, u32[]{:S(2)}, u32[]{:S(2)}) collective-permute-start(bf16[4,192,512]{2,1,0:T(8,128)(2,1)S(1)} %get-tuple-element.66), channel_id=1, source_target_pairs={{0,1},{1,0},{2,3},{3,2},{4,5},{5,4},{6,7},{7,6},{8,9},{9,8},{10,11... | collective-permute-start | bytes 2359304 | tf_op jit(solution)/shard_map/ppermute | solution.py:31
  86.2 16.3 %collective-permute-start.23 = (bf16[96,1408]{1,0:T(8,128)(2,1)S(1)}, bf16[96,1408]{1,0:T(8,128)(2,1)S(1)}, u32[]{:S(2)}, u32[]{:S(2)}) collective-permute-start(bf16[96,1408]{1,0:T(8,128)(2,1)S(1)} %fusion.3), channel_id=1, source_target_pairs={{0,2},{2,0},{4,6},{6,4},{8,10},{10,8},{12,14},{14,12},{1,3},{3,1},... | collective-permute-start | bytes 811016 | tf_op jit(solution)/shard_map/ppermute | solution.py:31
  87.3 16.7 %collective-permute-start.5 = (bf16[96,1408]{1,0:T(8,128)(2,1)S(1)}, bf16[96,1408]{1,0:T(8,128)(2,1)S(1)}, u32[]{:S(2)}, u32[]{:S(2)}) collective-permute-start(bf16[96,1408]{1,0:T(8,128)(2,1)S(1)} %collective-permute-done.4.refs_3_), channel_id=1, source_target_pairs={{0,16},{16,0},{1,17},{17,1},{2,18},{18,2},{3,19},{19,3},{4,20},{20... | collective-permute-start | bytes 811016 | tf_op jit(solution)/shard_map/ppermute | solution.py:31
  97.0 15.8 %collective-permute-start.26 = (bf16[192,1408]{1,0:T(8,128)(2,1)S(1)}, bf16[192,1408]{1,0:T(8,128)(2,1)S(1)}, u32[]{:S(2)}, u32[]{:S(2)}) collective-permute-start(bf16[192,1408]{1,0:T(8,128)(2,1)S(1)} %collective-permute-done.25.refs_3_), channel_id=1, source_target_pairs={{0,2},{2,0},{4,6},{6,4},{8,10},{10,8},{12,14},{14,12},{1,3},{3,1},... | collective-permute-start | bytes 1622024 | tf_op jit(solution)/shard_map/ppermute | solution.py:31
  110.7 16.6 %collective-permute-start.38 = (bf16[192,1408]{1,0:T(8,128)(2,1)S(1)}, bf16[192,1408]{1,0:T(8,128)(2,1)S(1)}, u32[]{:S(2)}, u32[]{:S(2)}) collective-permute-start(bf16[192,1408]{1,0:T(8,128)(2,1)S(1)} %get-tuple-element.86), channel_id=1, source_target_pairs={{0,4},{2,6},{4,0},{6,2},{8,12},{10,14},{12,8},{14,10},{1,5},{3,7},... | collective-permute-start | bytes 1622024 | tf_op jit(solution)/shard_map/ppermute | solution.py:31
  111.5 45.2 %collective-permute-start.37 = (bf16[192,1408]{1,0:T(8,128)(2,1)S(1)}, bf16[192,1408]{1,0:T(8,128)(2,1)S(1)}, u32[]{:S(2)}, u32[]{:S(2)}) collective-permute-start(bf16[192,1408]{1,0:T(8,128)(2,1)S(1)} %get-tuple-element.84), channel_id=1, source_target_pairs={{0,4},{2,6},{4,0},{6,2},{8,12},{10,14},{12,8},{14,10},{1,5},{3,7},... | collective-permute-start | bytes 1622024 | tf_op jit(solution)/shard_map/ppermute | solution.py:31
  120.1 20.2 %collective-permute-start.44 = (bf16[96,1408]{1,0:T(8,128)(2,1)S(1)}, bf16[96,1408]{1,0:T(8,128)(2,1)S(1)}, u32[]{:S(2)}, u32[]{:S(2)}) collective-permute-start(bf16[96,1408]{1,0:T(8,128)(2,1)S(1)} %get-tuple-element.92), channel_id=1, source_target_pairs={{0,2},{2,0},{4,6},{6,4},{8,10},{10,8},{12,14},{14,12},{1,3},{3,1},... | collective-permute-start | bytes 811016 | tf_op jit(solution)/shard_map/ppermute | solution.py:31
  129.1 15.5 %collective-permute-start.40 = (bf16[96,1408]{1,0:T(8,128)(2,1)S(1)}, bf16[96,1408]{1,0:T(8,128)(2,1)S(1)}, u32[]{:S(2)}, u32[]{:S(2)}) collective-permute-start(bf16[96,1408]{1,0:T(8,128)(2,1)S(1)} %get-tuple-element.88), channel_id=1, source_target_pairs={{0,2},{2,0},{4,6},{6,4},{8,10},{10,8},{12,14},{14,12},{1,3},{3,1},... | collective-permute-start | bytes 811016 | tf_op jit(solution)/shard_map/ppermute | solution.py:31
  140.2 15.5 %collective-permute-start.29 = (bf16[704,768]{1,0:T(8,128)(2,1)S(1)}, bf16[704,768]{1,0:T(8,128)(2,1)S(1)}, u32[]{:S(2)}, u32[]{:S(2)}) collective-permute-start(bf16[704,768]{1,0:T(8,128)(2,1)S(1)} %get-tuple-element.75), channel_id=1, source_target_pairs={{0,1},{1,0},{2,3},{3,2},{4,5},{5,4},{6,7},{7,6},{8,9},{9,8},{10,11... | collective-permute-start | bytes 3244040 | tf_op jit(solution)/shard_map/ppermute | solution.py:31
  140.3 17.6 %collective-permute-start.39 = (bf16[192,1408]{1,0:T(8,128)(2,1)S(1)}, bf16[192,1408]{1,0:T(8,128)(2,1)S(1)}, u32[]{:S(2)}, u32[]{:S(2)}) collective-permute-start(bf16[192,1408]{1,0:T(8,128)(2,1)S(1)} %add_convert_fusion.1), channel_id=1, source_target_pairs={{0,2},{2,0},{4,6},{6,4},{8,10},{10,8},{12,14},{14,12},{1,3},{3,1},... | collective-permute-start | bytes 1622024 | tf_op jit(solution)/shard_map/ppermute | solution.py:31
  141.4 14.1 %collective-permute-start.42 = (bf16[96,1408]{1,0:T(8,128)(2,1)S(1)}, bf16[96,1408]{1,0:T(8,128)(2,1)S(1)}, u32[]{:S(2)}, u32[]{:S(2)}) collective-permute-start(bf16[96,1408]{1,0:T(8,128)(2,1)S(1)} %add_convert_fusion.7), channel_id=1, source_target_pairs={{0,4},{2,6},{4,0},{6,2},{8,12},{10,14},{12,8},{14,10},{1,5},{3,7},... | collective-permute-start | bytes 811016 | tf_op jit(solution)/shard_map/ppermute | solution.py:31
  144.6 21.8 %collective-permute-start.47 = (bf16[96,1408]{1,0:T(8,128)(2,1)S(1)}, bf16[96,1408]{1,0:T(8,128)(2,1)S(1)}, u32[]{:S(2)}, u32[]{:S(2)}) collective-permute-start(bf16[96,1408]{1,0:T(8,128)(2,1)S(1)} %add_convert_fusion.3), channel_id=1, source_target_pairs={{0,8},{2,10},{4,12},{6,14},{8,0},{10,2},{12,4},{14,6},{1,9},{3,11}... | collective-permute-start | bytes 811016 | tf_op jit(solution)/shard_map/ppermute | solution.py:31
  (40 other events, 371.5 us)
